TPU v7x, 32 devices: a whole 2x2x4 slice. The times are simulated.
32 devices in a mesh: shard: 8 (over z, x), seq: 4 (over y, core).
Axes of the slice: x: 2, y: 2, z: 4, core: 2. Of those that a mesh axis runs over, the one named last changes fastest.
Arguments:
- tokens: bfloat16 [16, 2048, 768], P('shard', 'seq'), may hold values from -6 to 6
- cotangent: bfloat16 [16, 2048, 768], P('shard', 'seq'), may hold values from -6 to 6
- query_weight: bfloat16 [768, 768], P('shard'), may hold values from -0.21875 to 0.21875
- key_weight: bfloat16 [768, 768], P('shard'), may hold values from -0.21875 to 0.21875
- value_weight: bfloat16 [768, 768], P('shard'), may hold values from -0.21875 to 0.21875
- output_weight: bfloat16 [768, 768], P('shard'), may hold values from -0.875 to 0.875
- inner_weight: bfloat16 [768, 3072], P('shard'), may hold values from -0.21875 to 0.21875
- inner_bias: bfloat16 [3072], P('shard'), may hold values from -3 to 3
- outer_weight: bfloat16 [3072, 768], P('shard'), may hold values from -0.109375 to 0.109375
- first_gain: bfloat16 [768], P('shard'), may hold values from 0.25 to 1.75
- first_shift: bfloat16 [768], P('shard'), may hold values from -3 to 3
- second_gain: bfloat16 [768], P('shard'), may hold values from 0.25 to 1.75
- second_shift: bfloat16 [768], P('shard'), may hold values from -3 to 3
- doc_starts: int32 [16, 3], P('shard'), may hold values from 0 to 2047, as said below
- random_blocks: int32 [16, 32, 3], P('shard'), may hold values from 0 to 31
Outputs:
- layer_output: bfloat16 [16, 2048, 768], P('shard', 'seq')
- input_grad: bfloat16 [16, 2048, 768], P('shard', 'seq')
- query_grad: float32 [768, 768], P('shard')
- key_grad: float32 [768, 768], P('shard')
- value_grad: float32 [768, 768], P('shard')
- projection_grad: float32 [768, 768], P('shard')
- inner_grad: float32 [768, 3072], P('shard')
- inner_bias_grad: float32 [3072], P('shard')
- outer_grad: float32 [3072, 768], P('shard')
- first_gain_grad: float32 [768], P('shard')
- first_shift_grad: float32 [768], P('shard')
- second_gain_grad: float32 [768], P('shard')
- second_shift_grad: float32 [768], P('shard')
Inputs may be any that keep to these rules, and one draw needn't show every extreme that they name: `doc_starts`: each sequence has 3 distinct starts in increasing order, the first 0, all below 2048; the last start of the first sequence is 2047.
All inputs are finite; a program needn't handle non-finite values.
Results may differ from a plain program's by a relative error of at most 0.017.
Values may be sent and summed in bfloat16 or wider, within the bound.
No kernel may reach another device: no remote copies, remote signals or barrier semaphores. Data moves between devices by JAX's collectives and lax.ppermute only.
A program may use at most 320 MiB of HBM per device.

v0:
```python
import math

import jax
import jax.numpy as jnp
from jax import lax
from jax.sharding import PartitionSpec as P

H = 12
HD = 64
BLK = 64


EPS = 1e-06


def for_sending(array):

    def short(part):
        return part.astype(jnp.bfloat16) if part.dtype == jnp.float32 else part

    return jax.tree.map(short, array)


def layer_norm(values, gain, shift):
    centered = values - jnp.mean(values, axis=-1, keepdims=True)
    spread = jnp.mean(centered * centered, axis=-1, keepdims=True)
    return centered * lax.rsqrt(spread + EPS) * gain + shift


def activate(values):
    return jax.nn.gelu(values, approximate=True)


def block_mask(starts, chosen, seq_len, width):
    blocks = seq_len // width
    places = jnp.arange(seq_len, dtype=jnp.int32)
    segment = jnp.sum((starts[None, :] <= places[:, None]).astype(jnp.int32), axis=1)
    follow = jnp.concatenate([starts[1:], jnp.full((1,), seq_len, jnp.int32)])
    first_block = starts // width
    last_block = (follow - 1) // width
    numbers = jnp.arange(blocks, dtype=jnp.int32)
    special = jnp.any(first_block[None, :] == numbers[:, None], axis=1) | jnp.any(
        last_block[None, :] == numbers[:, None], axis=1
    )
    nearby = jnp.abs(numbers[:, None] - numbers[None, :]) <= 1
    picked = jnp.any(chosen[:, :, None] == numbers[None, None, :], axis=1)
    blocked = nearby | special[:, None] | special[None, :] | picked
    expanded = jnp.repeat(jnp.repeat(blocked, width, axis=0), width, axis=1)
    return expanded & (segment[:, None] == segment[None, :])


def body(
    tokens,
    cotangent,
    query_weight,
    key_weight,
    value_weight,
    output_weight,
    inner_weight,
    inner_bias,
    outer_weight,
    first_gain,
    first_shift,
    second_gain,
    second_shift,
    doc_starts,
    random_blocks,
):
    gathered = (
        lax.all_gather(query_weight, "shard", axis=0, tiled=True),
        lax.all_gather(key_weight, "shard", axis=0, tiled=True),
        lax.all_gather(value_weight, "shard", axis=0, tiled=True),
        lax.all_gather(output_weight, "shard", axis=0, tiled=True),
        lax.all_gather(inner_weight, "shard", axis=0, tiled=True),
        lax.all_gather(inner_bias, "shard", axis=0, tiled=True),
        lax.all_gather(outer_weight, "shard", axis=0, tiled=True),
        lax.all_gather(first_gain, "shard", axis=0, tiled=True),
        lax.all_gather(first_shift, "shard", axis=0, tiled=True),
        lax.all_gather(second_gain, "shard", axis=0, tiled=True),
        lax.all_gather(second_shift, "shard", axis=0, tiled=True),
    )
    (
        query_full,
        key_full,
        value_full,
        output_full,
        inner_full,
        bias_full,
        outer_full,
        gain_one,
        shift_one,
        gain_two,
        shift_two,
    ) = gathered
    width = query_full.shape[0]
    hidden = inner_full.shape[1]
    joined_weight = jnp.concatenate([query_full, key_full, value_full], axis=1)
    bias_float = bias_full.astype(jnp.float32)
    gain_one_f = gain_one.astype(jnp.float32)
    shift_one_f = shift_one.astype(jnp.float32)
    gain_two_f = gain_two.astype(jnp.float32)
    shift_two_f = shift_two.astype(jnp.float32)
    groups = lax.axis_size("seq")
    local_len = tokens.shape[1]
    seq_len = local_len * groups
    head_group = H // groups
    group_width = head_group * HD
    block_rows = min(512, seq_len)
    scale = 1.0 / math.sqrt(HD)

    def micro_step(totals, inputs):
        (
            acc_joined,
            acc_output,
            acc_inner,
            acc_bias,
            acc_outer,
            acc_gain_one,
            acc_shift_one,
            acc_gain_two,
            acc_shift_two,
        ) = totals
        row, grad_row, starts, chosen = inputs
        attend = block_mask(starts, chosen, seq_len, BLK)
        joined = jnp.dot(row, joined_weight, preferred_element_type=jnp.float32).astype(
            jnp.bfloat16
        )
        joined = joined.reshape(local_len, 3, groups, group_width)
        by_heads = lax.all_to_all(joined, "seq", split_axis=2, concat_axis=0, tiled=True).reshape(
            seq_len, 3, head_group, HD
        )
        queries = by_heads[:, 0]
        keys_all = by_heads[:, 1]
        values_all = by_heads[:, 2]

        def masked_scores(start):
            query_block = queries[start : start + block_rows]
            scores = (
                jnp.einsum(
                    "qhd,khd->hqk", query_block, keys_all, preferred_element_type=jnp.float32
                )
                * scale
            )
            return (
                query_block,
                jnp.where(attend[start : start + block_rows][None], scores, -1000000000.0),
            )

        contexts = []
        log_totals = []
        for start in range(0, seq_len, block_rows):
            query_block, scores = masked_scores(start)
            highest_score = jnp.max(scores, axis=-1, keepdims=True)
            expd = jnp.exp(scores - highest_score)
            denom = jnp.sum(expd, axis=-1, keepdims=True)
            probs = expd / denom
            log_totals.append(highest_score + jnp.log(denom))
            contexts.append(
                jnp.einsum(
                    "hqk,khd->qhd",
                    probs.astype(jnp.bfloat16),
                    values_all,
                    preferred_element_type=jnp.float32,
                ).astype(jnp.bfloat16)
            )
        context_heads = jnp.concatenate(contexts, axis=0).reshape(seq_len, 1, group_width)
        context = (
            lax.all_to_all(
                for_sending(context_heads), "seq", split_axis=0, concat_axis=1, tiled=True
            )
            .astype(context_heads.dtype)
            .reshape(local_len, width)
        )
        attended = jnp.dot(context, output_full, preferred_element_type=jnp.float32)
        res_one = row.astype(jnp.float32) + attended
        first = layer_norm(res_one, gain_one_f, shift_one_f)
        first_low = first.astype(jnp.bfloat16)
        inner = jnp.dot(first_low, inner_full, preferred_element_type=jnp.float32) + bias_float
        active = activate(inner).astype(jnp.bfloat16)
        outer = jnp.dot(active, outer_full, preferred_element_type=jnp.float32)
        res_two = first + outer
        result = layer_norm(res_two, gain_two_f, shift_two_f).astype(jnp.bfloat16)
        grad_float = grad_row.astype(jnp.float32)
        _, norm_two_back = jax.vjp(layer_norm, res_two, gain_two_f, shift_two_f)
        d_second, d_gain_two, d_shift_two = norm_two_back(grad_float)
        d_outer = d_second.astype(jnp.bfloat16)
        acc_outer = acc_outer + jnp.einsum(
            "ti,td->id", active, d_outer, preferred_element_type=jnp.float32
        )
        d_active = jnp.einsum("td,id->ti", d_outer, outer_full, preferred_element_type=jnp.float32)
        _, gelu_back = jax.vjp(activate, inner)
        d_inner = gelu_back(d_active)[0].astype(jnp.bfloat16)
        acc_bias = acc_bias + jnp.sum(d_inner.astype(jnp.float32), axis=0)
        acc_inner = acc_inner + jnp.einsum(
            "td,tf->df", first_low, d_inner, preferred_element_type=jnp.float32
        )
        d_first = d_second + jnp.einsum(
            "tf,df->td", d_inner, inner_full, preferred_element_type=jnp.float32
        )
        _, norm_one_back = jax.vjp(layer_norm, res_one, gain_one_f, shift_one_f)
        d_res, d_gain_one, d_shift_one = norm_one_back(d_first)
        d_attended = d_res.astype(jnp.bfloat16)
        acc_output = acc_output + jnp.einsum(
            "ti,td->id", context, d_attended, preferred_element_type=jnp.float32
        )
        d_context = jnp.einsum(
            "td,id->ti", d_attended, output_full, preferred_element_type=jnp.float32
        )
        d_context = d_context.astype(jnp.bfloat16).reshape(local_len, groups, group_width)
        d_heads = lax.all_to_all(d_context, "seq", split_axis=1, concat_axis=0, tiled=True).reshape(
            seq_len, head_group, HD
        )
        d_keys = jnp.zeros((seq_len, head_group, HD), jnp.float32)
        d_values = jnp.zeros((seq_len, head_group, HD), jnp.float32)
        d_query_blocks = []
        for index, start in enumerate(range(0, seq_len, block_rows)):
            query_block, scores = masked_scores(start)
            probs = jnp.exp(scores - log_totals[index])
            grad_block = d_heads[start : start + block_rows]
            d_probs = jnp.einsum(
                "qhd,khd->hqk", grad_block, values_all, preferred_element_type=jnp.float32
            )
            d_values = d_values + jnp.einsum(
                "hqk,qhd->khd",
                probs.astype(jnp.bfloat16),
                grad_block,
                preferred_element_type=jnp.float32,
            )
            centered = d_probs - jnp.sum(probs * d_probs, axis=-1, keepdims=True)
            d_scores = (probs * centered * scale).astype(jnp.bfloat16)
            d_query_blocks.append(
                jnp.einsum("hqk,khd->qhd", d_scores, keys_all, preferred_element_type=jnp.float32)
            )
            d_keys = d_keys + jnp.einsum(
                "hqk,qhd->khd", d_scores, query_block, preferred_element_type=jnp.float32
            )
        d_queries = jnp.concatenate(d_query_blocks, axis=0)
        d_joined = jnp.stack([d_queries, d_keys, d_values], axis=1).astype(jnp.bfloat16)
        d_joined = d_joined.reshape(seq_len, 3, 1, group_width)
        d_local = lax.all_to_all(d_joined, "seq", split_axis=0, concat_axis=2, tiled=True).reshape(
            local_len, 3 * width
        )
        acc_joined = acc_joined + jnp.einsum(
            "td,te->de", row, d_local, preferred_element_type=jnp.float32
        )
        d_input = d_res + jnp.einsum(
            "te,de->td", d_local, joined_weight, preferred_element_type=jnp.float32
        )
        updated = (
            acc_joined,
            acc_output,
            acc_inner,
            acc_bias,
            acc_outer,
            acc_gain_one + d_gain_one,
            acc_shift_one + d_shift_one,
            acc_gain_two + d_gain_two,
            acc_shift_two + d_shift_two,
        )
        return (updated, (result, d_input.astype(jnp.bfloat16)))

    starting = (
        jnp.zeros((width, 3 * width), jnp.float32),
        jnp.zeros((width, width), jnp.float32),
        jnp.zeros((width, hidden), jnp.float32),
        jnp.zeros((hidden,), jnp.float32),
        jnp.zeros((hidden, width), jnp.float32),
        jnp.zeros((width,), jnp.float32),
        jnp.zeros((width,), jnp.float32),
        jnp.zeros((width,), jnp.float32),
        jnp.zeros((width,), jnp.float32),
    )
    totals, (outputs, input_grads) = lax.scan(
        micro_step, starting, (tokens, cotangent, doc_starts, random_blocks)
    )
    (
        acc_joined,
        acc_output,
        acc_inner,
        acc_bias,
        acc_outer,
        acc_gain_one,
        acc_shift_one,
        acc_gain_two,
        acc_shift_two,
    ) = totals
    local_grads = (
        acc_joined[:, :width],
        acc_joined[:, width : 2 * width],
        acc_joined[:, 2 * width :],
        acc_output,
        acc_inner,
        acc_bias,
        acc_outer,
        acc_gain_one,
        acc_shift_one,
        acc_gain_two,
        acc_shift_two,
    )
    shares = (
        lax.psum_scatter(local_grads[0], "shard", scatter_dimension=0, tiled=True),
        lax.psum_scatter(local_grads[1], "shard", scatter_dimension=0, tiled=True),
        lax.psum_scatter(local_grads[2], "shard", scatter_dimension=0, tiled=True),
        lax.psum_scatter(local_grads[3], "shard", scatter_dimension=0, tiled=True),
        lax.psum_scatter(local_grads[4], "shard", scatter_dimension=0, tiled=True),
        lax.psum_scatter(local_grads[5], "shard", scatter_dimension=0, tiled=True),
        lax.psum_scatter(local_grads[6], "shard", scatter_dimension=0, tiled=True),
        lax.psum_scatter(local_grads[7], "shard", scatter_dimension=0, tiled=True),
        lax.psum_scatter(local_grads[8], "shard", scatter_dimension=0, tiled=True),
        lax.psum_scatter(local_grads[9], "shard", scatter_dimension=0, tiled=True),
        lax.psum_scatter(local_grads[10], "shard", scatter_dimension=0, tiled=True),
    )
    summed = (
        lax.psum(shares[0].astype(jnp.bfloat16), "seq").astype(jnp.float32),
        lax.psum(shares[1].astype(jnp.bfloat16), "seq").astype(jnp.float32),
        lax.psum(shares[2].astype(jnp.bfloat16), "seq").astype(jnp.float32),
        lax.psum(shares[3].astype(jnp.bfloat16), "seq").astype(jnp.float32),
        lax.psum(shares[4].astype(jnp.bfloat16), "seq").astype(jnp.float32),
        lax.psum(shares[5].astype(jnp.bfloat16), "seq").astype(jnp.float32),
        lax.psum(shares[6].astype(jnp.bfloat16), "seq").astype(jnp.float32),
        lax.psum(shares[7].astype(jnp.bfloat16), "seq").astype(jnp.float32),
        lax.psum(shares[8].astype(jnp.bfloat16), "seq").astype(jnp.float32),
        lax.psum(shares[9].astype(jnp.bfloat16), "seq").astype(jnp.float32),
        lax.psum(shares[10].astype(jnp.bfloat16), "seq").astype(jnp.float32),
    )
    return (
        outputs,
        input_grads,
        summed[0],
        summed[1],
        summed[2],
        summed[3],
        summed[4],
        summed[5],
        summed[6],
        summed[7],
        summed[8],
        summed[9],
        summed[10],
    )


def solution(mesh):
    placed = (
        P("shard", "seq", None),
        P("shard", "seq", None),
        P("shard", None),
        P("shard", None),
        P("shard", None),
        P("shard", None),
        P("shard", None),
        P("shard"),
        P("shard", None),
        P("shard"),
        P("shard"),
        P("shard"),
        P("shard"),
        P("shard", None),
        P("shard", None, None),
    )
    return jax.shard_map(
        body,
        mesh=mesh,
        in_specs=placed,
        out_specs=(
            P("shard", "seq", None),
            P("shard", "seq", None),
            P("shard", None),
            P("shard", None),
            P("shard", None),
            P("shard", None),
            P("shard", None),
            P("shard"),
            P("shard", None),
            P("shard"),
            P("shard"),
            P("shard"),
            P("shard"),
        ),
        check_vma=False,
    )
```

profile of v0, /device:TPU:0, one launch (start us, length us, event | category | flops | bytes accessed | tf_op | source)
XLA Modules:
  0.0 2124.0 jit_solution(12101311446130389150)
XLA Ops:
  41.4 26.0 %all-gather = bf16[8,1,384]{2,1,0:T(2,128)(2,1)S(1)} all-gather(bf16[1,1,384]{2,1,0:T(2,128)(2,1)S(1)} %reshape.380), channel_id=1, replica_groups=mesh['shard'=8,'seq'=4] {'shard'}, dimensions={0}, use_global_device_ids=true | all-gather | bytes 6912 | tf_op jit(solution)/shard_map/all_gather | solution.py:75
  67.5 28.6 %all-gather.10.cloned.1.call-done = bf16[768,768]{1,0:T(8,128)(2,1)} async-done(((bf16[96,768]{1,0:T(8,128)(2,1)}), bf16[768,768]{1,0:T(8,128)(2,1)}) %all-gather.10.cloned.1.call-update) | async-done | bytes 1179664 | tf_op jit(solution)/shard_map/all_gather | solution.py:71
  96.1 42.0 %all-gather.12.cloned.1.call-done = bf16[768,768]{1,0:T(8,128)(2,1)} async-done(((bf16[96,768]{1,0:T(8,128)(2,1)}), bf16[768,768]{1,0:T(8,128)(2,1)}) %all-gather.12.cloned.1.call-update) | async-done | bytes 1179664 | tf_op jit(solution)/shard_map/all_gather | solution.py:72
  141.4 38.6 %all-gather.14.cloned.1.call-done = bf16[768,768]{1,0:T(8,128)(2,1)} async-done(((bf16[96,768]{1,0:T(8,128)(2,1)}), bf16[768,768]{1,0:T(8,128)(2,1)}) %all-gather.14.cloned.1.call-update) | async-done | bytes 1179664 | tf_op jit(solution)/shard_map/all_gather | solution.py:73
  180.0 80.1 %all-gather.16.cloned.1.call-done = bf16[768,3072]{1,0:T(8,128)(2,1)} async-done(((bf16[96,3072]{1,0:T(8,128)(2,1)}), bf16[768,3072]{1,0:T(8,128)(2,1)}) %all-gather.16.cloned.1.call-update) | async-done | bytes 4718608 | tf_op jit(solution)/shard_map/all_gather | solution.py:74
  260.1 79.8 %all-gather.18.cloned.1.call-done = bf16[3072,768]{1,0:T(8,128)(2,1)} async-done(((bf16[384,768]{1,0:T(8,128)(2,1)}), bf16[3072,768]{1,0:T(8,128)(2,1)}) %all-gather.18.cloned.1.call-update) | async-done | bytes 4718608 | tf_op jit(solution)/shard_map/all_gather | solution.py:76
  339.8 1103.4 %while.34 = (s32[]{:T(128)}, f32[768,2304]{1,0:T(8,128)}, f32[768,768]{1,0:T(8,128)}, f32[768,3072]{1,0:T(8,128)}, f32[3072]{0:T(1024)}, /*index=5*/f32[3072,768...) while((s32[]{:T(128)}, f32[768,2304]{1,0:T(8,128)}, ...), condition=%wide.region_30.31_spmd.clone, body=%wide.region_0.30_spmd.clone.sunk | while | flops 32024104960 | bytes 1287496960 | solution.py:273
  573.9 27.8 %fusion.472 = f32[3,64,2048]{2,1,0:T(8,128)} fusion(f32[3,512,2048]{2,1,0:T(8,128)} %fusion.471, f32[3,512,2048]{2,1,0:T(8,128)} %get-tuple-element.919, f32[3,512]{1,0:T(4,128)S(1)} %log_add_fusion.10, pred[512,2048]{1,0:T(8,128)(4,1)} %copy.126, bf16[2048,3,3,64]{0,3,2,1:T(8,128)(2,1)S(1)} %copy-done.2), kind=kOutput, calls=%fused_computation.47.clone.1 | convolution fusion | flops 437259776 | bytes 54214656 | tf_op jit(solution)/shard_map/while/body/eval_jaxpr/hqk,qhd->khd/dot_general | solution.py:234
  669.8 23.9 %fusion.480 = bf16[512,3,64]{0,2,1:T(8,128)(2,1)} fusion(f32[3,512,2048]{2,1,0:T(8,128)} %fusion.475, f32[3,512,2048]{2,1,0:T(8,128)} %get-tuple-element.913, f32[3,512]{1,0:T(4,128)S(1)} %log_add_fusion.8, pred[512,2048]{1,0:T(8,128)(4,1)} %copy.124, bf16[2048,3,3,64]{0,3,2,1:T(8,128)(2,1)S(1)} %copy-done.2), kind=kOutput, calls=%fused_computation.158.clone.1 | convolution fusion | flops 437358080 | bytes 53428224 | tf_op jit(solution)/shard_map/while/body/eval_jaxpr/hqk,khd->qhd/dot_general | solution.py:232
  693.7 24.0 %fusion.481 = bf16[512,3,64]{0,2,1:T(8,128)(2,1)} fusion(f32[3,512,2048]{2,1,0:T(8,128)} %fusion.473, f32[3,512,2048]{2,1,0:T(8,128)} %get-tuple-element.916, f32[3,512]{1,0:T(4,128)S(1)} %log_add_fusion.9, pred[512,2048]{1,0:T(8,128)(4,1)} %copy.125, bf16[2048,3,3,64]{0,3,2,1:T(8,128)(2,1)S(1)} %copy-done.2), kind=kOutput, calls=%fused_computation.157.clone.1 | convolution fusion | flops 437358080 | bytes 53428224 | tf_op jit(solution)/shard_map/while/body/eval_jaxpr/hqk,khd->qhd/dot_general | solution.py:232
  717.7 25.7 %fusion.474 = f32[3,64,2048]{2,1,0:T(8,128)} fusion(f32[3,64,2048]{2,1,0:T(8,128)} %fusion.472, f32[3,512,2048]{2,1,0:T(8,128)} %fusion.473, f32[3,512,2048]{2,1,0:T(8,128)} %get-tuple-element.916, f32[3,512]{1,0:T(4,128)S(1)} %log_add_fusion.9, pred[512,2048]{1,0:T(8,128)(4,1)} %copy.125, bf16[2048,3,3,64]{0,3,2,1:T(8,128)(2,1)S(1)} %copy-done.2), kind=kOutput, calls=%fused_computation.118.clone.1 | convolution fusion | flops 437652992 | bytes 55787520 | tf_op jit(solution)/shard_map/while/body/eval_jaxpr/hqk,qhd->khd/dot_general | solution.py:234
  743.4 26.0 %fusion.476 = f32[3,64,2048]{2,1,0:T(8,128)} fusion(f32[3,64,2048]{2,1,0:T(8,128)} %fusion.474, f32[3,512,2048]{2,1,0:T(8,128)} %fusion.475, f32[3,512,2048]{2,1,0:T(8,128)} %get-tuple-element.913, f32[3,512]{1,0:T(4,128)S(1)} %log_add_fusion.8, pred[512,2048]{1,0:T(8,128)(4,1)} %copy.124, bf16[2048,3,3,64]{0,3,2,1:T(8,128)(2,1)S(1)} %copy-done.2), kind=kOutput, calls=%fused_computation.117.clone.1 | convolution fusion | flops 437652992 | bytes 55787520 | tf_op jit(solution)/shard_map/while/body/eval_jaxpr/hqk,qhd->khd/dot_general | solution.py:234
  830.7 35.7 %all-to-all-done.3 = bf16[2048,3,1,192]{3,1,2,0:T(4,128)(2,1)} async-done(((bf16[2048,3,1,192]{3,1,2,0:T(4,128)(2,1)}), bf16[2048,3,1,192]{3,1,2,0:T(4,128)(2,1)}, u32[]{:S(2)}, u32[]{:S(2)}) %all-to-all-start.3) | async-done | bytes 2359328 | tf_op jit(solution)/shard_map/while/body/eval_jaxpr/all_to_all | solution.py:240
  1124.3 28.0 %fusion.472 = f32[3,64,2048]{2,1,0:T(8,128)} fusion(f32[3,512,2048]{2,1,0:T(8,128)} %fusion.471, f32[3,512,2048]{2,1,0:T(8,128)} %get-tuple-element.919, f32[3,512]{1,0:T(4,128)S(1)} %log_add_fusion.10, pred[512,2048]{1,0:T(8,128)(4,1)} %copy.126, bf16[2048,3,3,64]{0,3,2,1:T(8,128)(2,1)S(1)} %copy-done.2), kind=kOutput, calls=%fused_computation.47.clone.1 | convolution fusion | flops 437259776 | bytes 54214656 | tf_op jit(solution)/shard_map/while/body/eval_jaxpr/hqk,qhd->khd/dot_general | solution.py:234
  1268.2 25.7 %fusion.474 = f32[3,64,2048]{2,1,0:T(8,128)} fusion(f32[3,64,2048]{2,1,0:T(8,128)} %fusion.472, f32[3,512,2048]{2,1,0:T(8,128)} %fusion.473, f32[3,512,2048]{2,1,0:T(8,128)} %get-tuple-element.916, f32[3,512]{1,0:T(4,128)S(1)} %log_add_fusion.9, pred[512,2048]{1,0:T(8,128)(4,1)} %copy.125, bf16[2048,3,3,64]{0,3,2,1:T(8,128)(2,1)S(1)} %copy-done.2), kind=kOutput, calls=%fused_computation.118.clone.1 | convolution fusion | flops 437652992 | bytes 55787520 | tf_op jit(solution)/shard_map/while/body/eval_jaxpr/hqk,qhd->khd/dot_general | solution.py:234
  1293.9 26.0 %fusion.476 = f32[3,64,2048]{2,1,0:T(8,128)} fusion(f32[3,64,2048]{2,1,0:T(8,128)} %fusion.474, f32[3,512,2048]{2,1,0:T(8,128)} %fusion.475, f32[3,512,2048]{2,1,0:T(8,128)} %get-tuple-element.913, f32[3,512]{1,0:T(4,128)S(1)} %log_add_fusion.8, pred[512,2048]{1,0:T(8,128)(4,1)} %copy.124, bf16[2048,3,3,64]{0,3,2,1:T(8,128)(2,1)S(1)} %copy-done.2), kind=kOutput, calls=%fused_computation.117.clone.1 | convolution fusion | flops 437652992 | bytes 55787520 | tf_op jit(solution)/shard_map/while/body/eval_jaxpr/hqk,qhd->khd/dot_general | solution.py:234
  1385.8 31.3 %all-to-all-done.3 = bf16[2048,3,1,192]{3,1,2,0:T(4,128)(2,1)} async-done(((bf16[2048,3,1,192]{3,1,2,0:T(4,128)(2,1)}), bf16[2048,3,1,192]{3,1,2,0:T(4,128)(2,1)}, u32[]{:S(2)}, u32[]{:S(2)}) %all-to-all-start.3) | async-done | bytes 2359328 | tf_op jit(solution)/shard_map/while/body/eval_jaxpr/all_to_all | solution.py:240
  1452.2 58.3 %reduce-scatter.13.cloned.1.call-done = f32[96,768]{1,0:T(8,128)} async-done(((f32[768,768]{1,0:T(8,128)}), f32[96,768]{1,0:T(8,128)}) %reduce-scatter.13.cloned.1.call-update) | async-done | bytes 294928 | tf_op jit(solution)/shard_map/reduce_scatter | solution.py:304
  1512.1 70.6 %reduce-scatter.11.cloned.1.call-done = f32[96,768]{1,0:T(8,128)} async-done(((f32[768,768]{1,0:T(8,128)}), f32[96,768]{1,0:T(8,128)}) %reduce-scatter.11.cloned.1.call-update) | async-done | bytes 294928 | tf_op jit(solution)/shard_map/reduce_scatter | solution.py:303
  1584.4 70.7 %reduce-scatter.7.cloned.1.call-done = f32[96,768]{1,0:T(8,128)} async-done(((f32[768,768]{1,0:T(8,128)}), f32[96,768]{1,0:T(8,128)}) %reduce-scatter.7.cloned.1.call-update) | async-done | bytes 294928 | tf_op jit(solution)/shard_map/reduce_scatter | solution.py:301
  1656.7 70.5 %reduce-scatter.9.cloned.1.call-done = f32[96,768]{1,0:T(8,128)} async-done(((f32[768,768]{1,0:T(8,128)}), f32[96,768]{1,0:T(8,128)}) %reduce-scatter.9.cloned.1.call-update) | async-done | bytes 294928 | tf_op jit(solution)/shard_map/reduce_scatter | solution.py:302
  1728.9 163.3 %reduce-scatter.15.cloned.1.call-done = f32[96,3072]{1,0:T(8,128)} async-done(((f32[768,3072]{1,0:T(8,128)}), f32[96,3072]{1,0:T(8,128)}) %reduce-scatter.15.cloned.1.call-update) | async-done | bytes 1179664 | tf_op jit(solution)/shard_map/reduce_scatter | solution.py:305
  1894.3 162.5 %reduce-scatter.17.cloned.1.call-done = f32[384,768]{1,0:T(8,128)} async-done(((f32[3072,768]{1,0:T(8,128)}), f32[384,768]{1,0:T(8,128)}) %reduce-scatter.17.cloned.1.call-update) | async-done | bytes 1179664 | tf_op jit(solution)/shard_map/reduce_scatter | solution.py:307
  2060.4 35.2 %all-reduce.9 = (bf16[3072]{0:T(1024)(128)(2,1)S(1)}, bf16[768]{0:T(1024)(128)(2,1)S(1)}, bf16[768]{0:T(1024)(128)(2,1)S(1)}, bf16[768]{0:T(1024)(128)(2,1)S(1)}, bf16[768]{0:T(1024)(128)(2,1)S(1)}) all-reduce(f32[3072]{0:T(1024)S(1)} %copy-done.26, f32[768]{0:T(1024)S(1)} %copy-done.40, ...), channel_id=7, replica_groups=mesh['shard'=8,'seq'=4] {'shard'}, use_global_device_ids=true, to_apply=%region_41.42.clone | all-reduce | flops 6144 | bytes 36864
  (514 shorter events, 902.6 us)
Async XLA Ops:
  7.2 60.3 %all-gather.8.cloned.1.call-start = ((), (), s32[]{:S(2)}) async-start(), calls=%async_computation.10 | async-start | bytes 1327104 | tf_op jit(solution)/shard_map/all_gather | solution.py:70
  7.9 88.2 %all-gather.10.cloned.1.call-start = ((), (), s32[]{:S(2)}) async-start(), calls=%async_computation.11 | async-start | bytes 1327104 | tf_op jit(solution)/shard_map/all_gather | solution.py:71
  8.7 129.4 %all-gather.12.cloned.1.call-start = ((), (), s32[]{:S(2)}) async-start(), calls=%async_computation.12 | async-start | bytes 1327104 | tf_op jit(solution)/shard_map/all_gather | solution.py:72
  9.4 170.6 %all-gather.14.cloned.1.call-start = ((), (), s32[]{:S(2)}) async-start(), calls=%async_computation.13 | async-start | bytes 1327104 | tf_op jit(solution)/shard_map/all_gather | solution.py:73
  10.0 250.1 %all-gather.16.cloned.1.call-start = ((), (), s32[]{:S(2)}) async-start(), calls=%async_computation.14 | async-start | bytes 5308416 | tf_op jit(solution)/shard_map/all_gather | solution.py:74
  10.6 329.3 %all-gather.18.cloned.1.call-start = ((), (), s32[]{:S(2)}) async-start(), calls=%async_computation.15 | async-start | bytes 5308416 | tf_op jit(solution)/shard_map/all_gather | solution.py:76
  11.1 1499.4 %reduce-scatter.13.cloned.1.call-start = ((), (), s32[]{:S(2)}) async-start(), calls=%async_computation.19 | async-start | bytes 2654208 | tf_op jit(solution)/shard_map/reduce_scatter | solution.py:304
  350.1 32.1 %all-to-all-start = ((bf16[512,3,4,192]{0,3,1,2:T(8,128)(2,1)}), bf16[512,3,4,192]{0,3,1,2:T(8,128)(2,1)S(1)}, u32[]{:S(2)}, u32[]{:S(2)}) async-start(bf16[512,3,4,192]{0,3,1,2:T(8,128)(2,1)} %copy.122), calls=%async_computation | async-start | bytes 4718592 | tf_op jit(solution)/shard_map/while/body/eval_jaxpr/all_to_all | solution.py:129
  474.8 15.1 all-to-all-start.1
  524.8 15.9 all-to-all-start.2
  813.0 53.4 %all-to-all-start.3 = ((bf16[2048,3,1,192]{3,1,2,0:T(4,128)(2,1)}), bf16[2048,3,1,192]{3,1,2,0:T(4,128)(2,1)}, u32[]{:S(2)}, u32[]{:S(2)}) async-start(bf16[2048,3,1,192]{3,1,2,0:T(4,128)(2,1)} %pad_maximum_fusion.9), calls=%async_computation.3 | async-start | bytes 8388608 | tf_op jit(solution)/shard_map/while/body/eval_jaxpr/all_to_all | solution.py:240
  900.7 32.1 %all-to-all-start = ((bf16[512,3,4,192]{0,3,1,2:T(8,128)(2,1)}), bf16[512,3,4,192]{0,3,1,2:T(8,128)(2,1)S(1)}, u32[]{:S(2)}, u32[]{:S(2)}) async-start(bf16[512,3,4,192]{0,3,1,2:T(8,128)(2,1)} %copy.122), calls=%async_computation | async-start | bytes 4718592 | tf_op jit(solution)/shard_map/while/body/eval_jaxpr/all_to_all | solution.py:129
  1025.4 15.1 all-to-all-start.1
  1075.3 15.9 all-to-all-start.2
  1363.7 53.3 %all-to-all-start.3 = ((bf16[2048,3,1,192]{3,1,2,0:T(4,128)(2,1)}), bf16[2048,3,1,192]{3,1,2,0:T(4,128)(2,1)}, u32[]{:S(2)}, u32[]{:S(2)}) async-start(bf16[2048,3,1,192]{3,1,2,0:T(4,128)(2,1)} %pad_maximum_fusion.9), calls=%async_computation.3 | async-start | bytes 8388608 | tf_op jit(solution)/shard_map/while/body/eval_jaxpr/all_to_all | solution.py:240
  1443.2 139.6 %reduce-scatter.11.cloned.1.call-start = ((), (), s32[]{:S(2)}) async-start(), calls=%async_computation.18 | async-start | bytes 2654208 | tf_op jit(solution)/shard_map/reduce_scatter | solution.py:303
  1449.5 205.6 %reduce-scatter.7.cloned.1.call-start = ((), (), s32[]{:S(2)}) async-start(), calls=%async_computation.16 | async-start | bytes 2654208 | tf_op jit(solution)/shard_map/reduce_scatter | solution.py:301
  1450.3 277.0 %reduce-scatter.9.cloned.1.call-start = ((), (), s32[]{:S(2)}) async-start(), calls=%async_computation.17 | async-start | bytes 2654208 | tf_op jit(solution)/shard_map/reduce_scatter | solution.py:302
  1450.8 441.3 %reduce-scatter.15.cloned.1.call-start = ((), (), s32[]{:S(2)}) async-start(), calls=%async_computation.20 | async-start | bytes 10616832 | tf_op jit(solution)/shard_map/reduce_scatter | solution.py:305
  1451.6 605.3 %reduce-scatter.17.cloned.1.call-start = ((), (), s32[]{:S(2)}) async-start(), calls=%async_computation.21 | async-start | bytes 10616832 | tf_op jit(solution)/shard_map/reduce_scatter | solution.py:307
  1451.6 608.7 %copy-start.26 = (f32[3072]{0:T(1024)S(1)}, f32[3072]{0:T(1024)}, u32[]{:S(2)}) copy-start(f32[3072]{0:T(1024)} %get-tuple-element.396) | copy-start | bytes 36868
  1451.6 608.7 %copy-start.31 = (f32[768]{0:T(1024)S(1)}, f32[768]{0:T(1024)}, u32[]{:S(2)}) copy-start(f32[768]{0:T(1024)} %get-tuple-element.401) | copy-start | bytes 9220
  1451.6 608.7 %copy-start.34 = (f32[768]{0:T(1024)S(1)}, f32[768]{0:T(1024)}, u32[]{:S(2)}) copy-start(f32[768]{0:T(1024)} %get-tuple-element.400) | copy-start | bytes 9220
  1452.2 654.1 %all-reduce.15.cloned.1.call-start = ((), (), s32[]{:S(2)}) async-start(), calls=%async_computation.22 | async-start | bytes 3538944 | tf_op jit(solution)/shard_map/psum | solution.py:314
  (102 other events, 2472.0 us)
Sparse Core Ops, SparseCore 0:
  10.2 43.8 all-gather.7
  56.2 39.8 all-gather.9
  98.3 39.8 all-gather.11
  140.1 39.8 all-gather.13
  182.0 78.0 all-gather.15
  262.1 77.6 all-gather.17
  1443.3 67.1 reduce-scatter.12
  1514.0 68.7 reduce-scatter.10
  1586.3 68.7 reduce-scatter.6
  1658.4 68.7 reduce-scatter.8
  1730.8 161.3 reduce-scatter.14
  1895.6 161.1 reduce-scatter.16
  2060.8 45.3 all-reduce.14
where the time goes:
time: 2130 us; the launch traced here: 2120 us
  waiting for transfers between devices  973 us (46%)
  matrix products  720 us (34%)
  local copies, waits for them, and re-layouts  156 us (7%)
  other arithmetic  130 us (6%)
  blocking collectives  91.2 us (4%)
  starting transfers between devices  33.5 us (2%)
    dot_general x8, matrix products, micro_step(): jnp.einsum('hqk,qhd->khd', d_scores, query_block, preferred_element_type=...  204 us
    dot_general x8, matrix products, micro_step(): jnp.einsum('hqk,khd->qhd', d_scores, keys_all, preferred_element_type=jnp...  184 us
    reduce_scatter x1, waiting for transfers between devices, body(): lax.psum_scatter(local_grads[4], 'shard', scatter_dimension=0, tiled=True)  163 us
    reduce_scatter x1, waiting for transfers between devices, body(): lax.psum_scatter(local_grads[6], 'shard', scatter_dimension=0, tiled=True)  163 us
    all_gather x1, waiting for transfers between devices, body(): lax.all_gather(inner_weight, 'shard', axis=0, tiled=True)  80.1 us
    all_gather x1, waiting for transfers between devices, body(): lax.all_gather(outer_weight, 'shard', axis=0, tiled=True)  79.8 us
    reduce_scatter x1, waiting for transfers between devices, body(): lax.psum_scatter(local_grads[0], 'shard', scatter_dimension=0, tiled=True)  70.7 us
    reduce_scatter x1, waiting for transfers between devices, body(): lax.psum_scatter(local_grads[2], 'shard', scatter_dimension=0, tiled=True)  70.6 us
  transfers between devices with their start and end apart: 21, of which 20 were waited for; matrix products, arithmetic and copies ran while one was open for 6% of the time, Pallas kernels for 0%

commit v1 on v0

v1 whole, which is shorter than its diff:
```python
import jax
import jax.numpy as jnp
from jax import lax
from jax.experimental import pallas as pl
from jax.experimental.pallas import tpu as pltpu
from jax.sharding import PartitionSpec as P

H = 12
HD = 64
EPS = 1e-06
BLK=64; PAIR=128; GRP=4
F32=jnp.float32; BF=jnp.bfloat16

def nt(a,b): return lax.dot_general(a,b,(((1,),(1,)),((),())),preferred_element_type=F32)
def tn(a,b): return lax.dot_general(a,b,(((0,),(0,)),((),())),preferred_element_type=F32)
def nn(a,b): return lax.dot_general(a,b,(((1,),(0,)),((),())),preferred_element_type=F32)

def fwd_call(mine, recv, qmask, kmask, idx, cnt):
    half=mine.shape[0]; seq=2*half; nb=seq//BLK; width=mine.shape[1]//3; pairs=width//PAIR
    rows=2*BLK; gk=GRP*BLK; maxg=nb//GRP
    def kern(idx_ref,cnt_ref,mine_ref,recv_ref,qm_ref,km_ref,out_ref,log_ref,kx,vx,s_scr,mx,acc,ls):
        lane=lax.broadcasted_iota(jnp.int32,(BLK,PAIR),1)
        low=lane<BLK
        for p in range(pairs):
            for t,src in ((0,mine_ref),(1,recv_ref)):
                kx[p,t*half:(t+1)*half,:PAIR]=src[:,width+p*PAIR:width+(p+1)*PAIR]
                vx[p,t*half:(t+1)*half,:]=src[:,2*width+p*PAIR:2*width+(p+1)*PAIR]
            kx[p,seq:seq+BLK,:PAIR]=jnp.zeros((BLK,PAIR),BF)
            vx[p,seq:seq+BLK,:]=jnp.zeros((BLK,PAIR),BF)
            kx[p,:,PAIR:]=km_ref[...]
        def half_loop(src_ref,base):
            def qblock(b,_):
                i=base+b
                n=cnt_ref[i]
                qrow=pl.multiple_of(b*BLK,BLK)
                qm=qm_ref[pl.ds(pl.multiple_of(i*BLK,BLK),BLK),:]
                qs=[]
                for p in range(pairs):
                    q=src_ref[pl.ds(qrow,BLK),p*PAIR:(p+1)*PAIR]*jnp.asarray(0.125,BF)
                    z=jnp.zeros_like(q)
                    stk=jnp.concatenate([jnp.where(low,q,z),jnp.where(low,z,q)],axis=0)
                    qs.append(jnp.concatenate([stk,jnp.concatenate([qm,qm],axis=0)],axis=1))
                    mx[p]=jnp.full((rows,PAIR),-3e38,F32)
                    ls[p]=jnp.zeros((rows,PAIR),F32)
                    acc[p]=jnp.zeros((rows,PAIR),F32)
                def p1(g,_):
                    at=[pl.multiple_of(idx_ref[i,g*GRP+j]*BLK,BLK) for j in range(GRP)]
                    for p in range(pairs):
                        kg=jnp.concatenate([kx[p,pl.ds(a,BLK),:] for a in at],axis=0)
                        s=nt(qs[p],kg)
                        s_scr[g,p]=s
                        mx[p]=jnp.maximum(mx[p],jnp.maximum(s[:,:PAIR],s[:,PAIR:]))
                    return 0
                lax.fori_loop(0,n,p1,0)
                ms=[jnp.max(mx[p],axis=1,keepdims=True) for p in range(pairs)]
                def p2(g,_):
                    at=[pl.multiple_of(idx_ref[i,g*GRP+j]*BLK,BLK) for j in range(GRP)]
                    for p in range(pairs):
                        vg=jnp.concatenate([vx[p,pl.ds(a,BLK),:] for a in at],axis=0)
                        e=jnp.exp(s_scr[g,p]-ms[p])
                        ls[p]=ls[p]+(e[:,:PAIR]+e[:,PAIR:])
                        acc[p]=acc[p]+nn(e.astype(BF),vg)
                    return 0
                lax.fori_loop(0,n,p2,0)
                lanes=lax.broadcasted_iota(jnp.int32,(rows,PAIR),1)
                logs=jnp.zeros((rows,PAIR),F32)
                for p in range(pairs):
                    l=jnp.sum(ls[p],axis=1,keepdims=True)
                    o=acc[p]*(1.0/l)
                    o=jnp.where(low,o[:BLK],o[BLK:])
                    out_ref[pl.ds(pl.multiple_of(i*BLK,BLK),BLK),p*PAIR:(p+1)*PAIR]=o.astype(BF)
                    logs=jnp.where(lanes==p,ms[p]+jnp.log(l),logs)
                log_ref[pl.ds(pl.multiple_of(i*rows,rows),rows),:]=logs
                return 0
            lax.fori_loop(0,nb//2,qblock,0)
        half_loop(mine_ref,0)
        half_loop(recv_ref,nb//2)
    v=pl.BlockSpec(memory_space=pltpu.VMEM)
    s=pl.BlockSpec(memory_space=pltpu.SMEM)
    return pl.pallas_call(kern,name="attn_fwd",
        out_shape=(jax.ShapeDtypeStruct((seq,width),BF),jax.ShapeDtypeStruct((nb*rows,PAIR),F32)),
        in_specs=[s,s,v,v,v,v],out_specs=(v,v),
        scratch_shapes=[pltpu.VMEM((pairs,seq+BLK,2*PAIR),BF),pltpu.VMEM((pairs,seq+BLK,PAIR),BF),
            pltpu.VMEM((maxg,pairs,rows,gk),F32),pltpu.VMEM((pairs,rows,PAIR),F32),pltpu.VMEM((pairs,rows,PAIR),F32),pltpu.VMEM((pairs,rows,PAIR),F32)],
        cost_estimate=pl.CostEstimate(flops=20_000_000_000,transcendentals=12_000_000,bytes_accessed=12_000_000),
    )(idx,cnt,mine,recv,qmask,kmask)

def bwd_call(mine, recv, dmine, drecv, out, logs, qmask, kmask, idx, cnt):
    half=mine.shape[0]; seq=2*half; nb=seq//BLK; width=mine.shape[1]//3; pairs=width//PAIR
    rows=2*BLK; gk=GRP*BLK
    def kern(idx_ref,cnt_ref,mine_ref,recv_ref,dm_ref,dr_ref,o_ref,log_ref,qm_ref,km_ref,g_ref,kx,vx,dk,dv,dq):
        lane=lax.broadcasted_iota(jnp.int32,(BLK,PAIR),1)
        low=lane<BLK
        for p in range(pairs):
            for t,src in ((0,mine_ref),(1,recv_ref)):
                kx[p,t*half:(t+1)*half,:PAIR]=src[:,width+p*PAIR:width+(p+1)*PAIR]
                vx[p,t*half:(t+1)*half,:]=src[:,2*width+p*PAIR:2*width+(p+1)*PAIR]
            kx[p,seq:seq+BLK,:PAIR]=jnp.zeros((BLK,PAIR),BF)
            vx[p,seq:seq+BLK,:]=jnp.zeros((BLK,PAIR),BF)
            kx[p,:,PAIR:]=km_ref[...]
            dk[p]=jnp.zeros((seq+BLK,PAIR),F32)
            dv[p]=jnp.zeros((seq+BLK,PAIR),F32)
        def half_loop(src_ref,dsrc_ref,base):
            def qblock(b,_):
                i=base+b
                n=cnt_ref[i]
                qrow=pl.multiple_of(b*BLK,BLK)
                irow=pl.multiple_of(i*BLK,BLK)
                qm=qm_ref[pl.ds(irow,BLK),:]
                logs=log_ref[pl.ds(pl.multiple_of(i*rows,rows),rows),:]
                qs=[];ds_=[];ls_=[];dl=[]
                for p in range(pairs):
                    q=src_ref[pl.ds(qrow,BLK),p*PAIR:(p+1)*PAIR]*jnp.asarray(0.125,BF)
                    z=jnp.zeros_like(q)
                    stk=jnp.concatenate([jnp.where(low,q,z),jnp.where(low,z,q)],axis=0)
                    qs.append(jnp.concatenate([stk,jnp.concatenate([qm,qm],axis=0)],axis=1))
                    d=dsrc_ref[pl.ds(qrow,BLK),p*PAIR:(p+1)*PAIR]
                    ds_.append(jnp.concatenate([jnp.where(low,d,z),jnp.where(low,z,d)],axis=0))
                    prod=d.astype(F32)*o_ref[pl.ds(irow,BLK),p*PAIR:(p+1)*PAIR].astype(F32)
                    zf=jnp.zeros_like(prod)
                    dl.append(jnp.sum(jnp.concatenate([jnp.where(low,prod,zf),jnp.where(low,zf,prod)],axis=0),axis=1,keepdims=True))
                    ls_.append(logs[:,p:p+1])
                    dq[p]=jnp.zeros((rows,PAIR),F32)
                def step(g,_):
                    at=[pl.multiple_of(idx_ref[i,g*GRP+j]*BLK,BLK) for j in range(GRP)]
                    for p in range(pairs):
                        kg=jnp.concatenate([kx[p,pl.ds(a,BLK),:] for a in at],axis=0)
                        vg=jnp.concatenate([vx[p,pl.ds(a,BLK),:] for a in at],axis=0)
                        s=nt(qs[p],kg)
                        e=jnp.exp(s-ls_[p])
                        dp=nt(ds_[p],vg)
                        dsc=(e*(dp-dl[p])).astype(BF)
                        dq[p]=dq[p]+nn(dsc,kg[:,:PAIR])
                        dkg=tn(dsc,qs[p][:,:PAIR])
                        dvg=tn(e.astype(BF),ds_[p])
                        for j,a in enumerate(at):
                            dk[p,pl.ds(a,BLK),:]=dk[p,pl.ds(a,BLK),:]+dkg[j*BLK:(j+1)*BLK]
                            dv[p,pl.ds(a,BLK),:]=dv[p,pl.ds(a,BLK),:]+dvg[j*BLK:(j+1)*BLK]
                    return 0
                lax.fori_loop(0,n,step,0)
                for p in range(pairs):
                    g=dq[p]
                    g_ref[pl.ds(irow,BLK),p*PAIR:(p+1)*PAIR]=(jnp.where(low,g[:BLK],g[BLK:])*0.125).astype(BF)
                return 0
            lax.fori_loop(0,nb//2,qblock,0)
        half_loop(mine_ref,dm_ref,0)
        half_loop(recv_ref,dr_ref,nb//2)
        for p in range(pairs):
            g_ref[:,width+p*PAIR:width+(p+1)*PAIR]=dk[p,:seq].astype(BF)
            g_ref[:,2*width+p*PAIR:2*width+(p+1)*PAIR]=dv[p,:seq].astype(BF)
    v=pl.BlockSpec(memory_space=pltpu.VMEM)
    s=pl.BlockSpec(memory_space=pltpu.SMEM)
    return pl.pallas_call(kern,name="attn_bwd",
        out_shape=jax.ShapeDtypeStruct((seq,3*width),BF),
        in_specs=[s,s,v,v,v,v,v,v,v,v],out_specs=v,
        scratch_shapes=[pltpu.VMEM((pairs,seq+BLK,2*PAIR),BF),pltpu.VMEM((pairs,seq+BLK,PAIR),BF),
            pltpu.VMEM((pairs,seq+BLK,PAIR),F32),pltpu.VMEM((pairs,seq+BLK,PAIR),F32),pltpu.VMEM((pairs,rows,PAIR),F32)],
        cost_estimate=pl.CostEstimate(flops=50_000_000_000,transcendentals=12_000_000,bytes_accessed=18_000_000),
    )(idx,cnt,mine,recv,dmine,drecv,out,logs,qmask,kmask)

def tables(starts, chosen, orig, seq):
    nb=orig.shape[0]
    follow=jnp.concatenate([starts[1:],jnp.full((1,),seq,jnp.int32)])-1
    fb=starts//BLK; lb=follow//BLK
    special=jnp.any(fb[None,:]==orig[:,None],axis=1)|jnp.any(lb[None,:]==orig[:,None],axis=1)
    nearby=jnp.abs(orig[:,None]-orig[None,:])<=1
    picked=jnp.any(chosen[:,:,None]==orig[None,None,:],axis=1)
    allowed=nearby|special[:,None]|special[None,:]|picked
    lo=jnp.sum((starts[None,:]<=(orig*BLK)[:,None]).astype(jnp.int32),axis=1)
    hi=jnp.sum((starts[None,:]<=(orig*BLK+BLK-1)[:,None]).astype(jnp.int32),axis=1)
    allowed=allowed&(lo[:,None]<=hi[None,:])&(lo[None,:]<=hi[:,None])
    a=allowed.astype(jnp.int32)
    before=jnp.arange(nb)
    rank=jnp.sum(jnp.where((before[None,:]<before[:,None])[None],a[:,None,:],0),axis=2)
    hit=(rank[:,:,None]==before[None,None,:])&allowed[:,:,None]
    idx=nb+jnp.sum(jnp.where(hit,before[None,:,None]-nb,0),axis=1)
    cnt=(jnp.sum(a,axis=1)+GRP-1)//GRP
    pos=(orig[:,None]*BLK+jnp.arange(BLK)[None,:]).reshape(-1)
    seg=jnp.sum((starts[None,:]<=pos[:,None]).astype(jnp.int32),axis=1)-1
    col=jnp.arange(PAIR)[None,:]
    nd=starts.shape[0]
    qmask=jnp.where((col<=nd)&(col!=seg[:,None]),-1e9,0.0).astype(BF)
    kseg=jnp.concatenate([seg,jnp.full((BLK,),nd,jnp.int32)])
    kmask=(col==kseg[:,None]).astype(BF)
    return idx.astype(jnp.int32),cnt.astype(jnp.int32),qmask,kmask


def swap(value, flip, groups):
    return lax.ppermute(value, "seq", [(s, s ^ flip) for s in range(groups)])


def halves(full, c, width):
    parts = full.reshape(full.shape[0], -1, 2, width)
    own = lax.dynamic_index_in_dim(parts, c, 2, keepdims=False)
    other = lax.dynamic_index_in_dim(parts, 1 - c, 2, keepdims=False)
    return own.reshape(full.shape[0], -1), other.reshape(full.shape[0], -1)


def join(own, other, c, width):
    a = own.reshape(own.shape[0], -1, 1, width)
    b = other.reshape(other.shape[0], -1, 1, width)
    both = jnp.where(c == 0, jnp.concatenate([a, b], 2), jnp.concatenate([b, a], 2))
    return both.reshape(own.shape[0], -1)


def gather_rows(local, s, groups):
    part = local.shape[0] // groups
    mine = lax.dynamic_slice_in_dim(local, s * part, part, 0)
    return lax.all_gather(mine, ("shard", "seq"), axis=0, tiled=True)


def scatter_rows(grad):
    share = lax.psum_scatter(grad.astype(BF), ("shard", "seq"), scatter_dimension=0, tiled=True)
    return lax.all_gather(share, "seq", axis=0, tiled=True).astype(F32)


def body(tokens, cotangent, query_weight, key_weight, value_weight, output_weight, inner_weight,
         inner_bias, outer_weight, first_gain, first_shift, second_gain, second_shift, doc_starts, random_blocks):
    groups = lax.axis_size("seq")
    shards = lax.axis_size("shard")
    rows, local, width = tokens.shape
    assert rows == 2 and groups == 4
    seq = local * groups
    s = lax.axis_index("seq")
    c = s % 2
    y = s // 2
    flip = 2
    hw = (H // 2) * HD

    def bring(pair):
        own = lax.dynamic_index_in_dim(pair, y, 0, keepdims=False)
        away = swap(lax.dynamic_index_in_dim(pair, 1 - y, 0, keepdims=False), flip, groups)
        return jnp.concatenate([own, away], axis=0)

    def give_back(value):
        own = value[:local]
        away = swap(value[local:], flip, groups)
        return jnp.where(y == 0, jnp.stack([own, away]), jnp.stack([away, own]))

    x = bring(tokens)
    cot = bring(cotangent).astype(F32)
    joined_local = jnp.concatenate([query_weight, key_weight, value_weight], axis=1)
    joined = gather_rows(joined_local, s, groups)
    small_local = jnp.concatenate([inner_bias, first_gain, first_shift, second_gain, second_shift])
    small = lax.all_gather(small_local, "shard", axis=0, tiled=False).astype(F32)
    output_full = gather_rows(output_weight, s, groups)
    inner_full = gather_rows(inner_weight, s, groups)
    outer_full = gather_rows(outer_weight, s, groups)
    cuts = [0]
    for item in (inner_bias, first_gain, first_shift, second_gain, second_shift):
        cuts.append(cuts[-1] + item.shape[0])
    bias, gain_one, shift_one, gain_two, shift_two = [
        small[:, a:b].reshape(-1) for a, b in zip(cuts[:-1], cuts[1:])
    ]

    nb = seq // BLK
    per = nb // groups
    quarters = jnp.stack([s, s ^ 2, s ^ 1, s ^ 3])
    orig = (quarters[:, None] * per + jnp.arange(per)[None, :]).reshape(-1).astype(jnp.int32)
    starts = lax.dynamic_index_in_dim(doc_starts, y, 0, keepdims=False)
    chosen = lax.dynamic_index_in_dim(random_blocks, y, 0, keepdims=False)
    chosen = jnp.sum(jnp.where((orig[:, None] == jnp.arange(nb)[None, :])[:, :, None], chosen[None], 0), axis=1)
    idx, cnt, qmask, kmask = tables(starts, chosen, orig, seq)

    w_own, w_sib = halves(joined, c, hw)
    sib_qkv = nn(x, w_sib).astype(BF)
    recv_qkv = swap(sib_qkv, 1, groups)
    own_qkv = nn(x, w_own).astype(BF)
    context_all, logs = fwd_call(own_qkv, recv_qkv, qmask, kmask, idx, cnt)
    ctx_own = context_all[: 2 * local]
    ctx_sib = swap(context_all[2 * local :], 1, groups)
    context = join(ctx_own, ctx_sib, c, hw)
    attended = nn(context, output_full)
    res_one = x.astype(F32) + attended
    cen = res_one - jnp.mean(res_one, axis=-1, keepdims=True)
    rstd_one = lax.rsqrt(jnp.mean(cen * cen, axis=-1, keepdims=True) + EPS)
    n_one = cen * rstd_one
    first = n_one * gain_one + shift_one
    first_low = first.astype(BF)
    inner = nn(first_low, inner_full) + bias
    root = 0.7978845608028654
    tanh = jnp.tanh(root * (inner + 0.044715 * inner * inner * inner))
    active = (0.5 * inner * (1.0 + tanh)).astype(BF)
    slope = 0.5 * (1.0 + tanh) + 0.5 * inner * (1.0 - tanh * tanh) * root * (1.0 + 3 * 0.044715 * inner * inner)
    outer = nn(active, outer_full)
    res_two = first + outer
    cen2 = res_two - jnp.mean(res_two, axis=-1, keepdims=True)
    rstd_two = lax.rsqrt(jnp.mean(cen2 * cen2, axis=-1, keepdims=True) + EPS)
    n_two = cen2 * rstd_two
    result = give_back((n_two * gain_two + shift_two).astype(BF))
    g_two = cot * gain_two
    d_second = (g_two - jnp.mean(g_two, -1, keepdims=True) - n_two * jnp.mean(g_two * n_two, -1, keepdims=True)) * rstd_two
    d_gain_two = jnp.sum(cot * n_two, axis=0)
    d_shift_two = jnp.sum(cot, axis=0)
    d_outer = d_second.astype(BF)
    outer_grad = scatter_rows(tn(active, d_outer))
    d_inner = (nt(d_outer, outer_full) * slope).astype(BF)
    d_bias = jnp.sum(d_inner.astype(F32), axis=0)
    inner_grad = scatter_rows(tn(first_low, d_inner))
    d_first = d_second + nt(d_inner, inner_full)
    d_gain_one = jnp.sum(d_first * n_one, axis=0)
    d_shift_one = jnp.sum(d_first, axis=0)
    k_one = d_first * gain_one
    d_res = (k_one - jnp.mean(k_one, -1, keepdims=True) - n_one * jnp.mean(k_one * n_one, -1, keepdims=True)) * rstd_one
    d_attended = d_res.astype(BF)
    projection_grad = scatter_rows(tn(context, d_attended))
    d_context = nt(d_attended, output_full).astype(BF)
    dc_own, dc_sib = halves(d_context, c, hw)
    dc_recv = swap(dc_sib, 1, groups)
    d_qkv = bwd_call(own_qkv, recv_qkv, dc_own, dc_recv, context_all, logs, qmask, kmask, idx, cnt)
    d_own = d_qkv[: 2 * local]
    d_sib = swap(d_qkv[2 * local :], 1, groups)
    d_input = d_res + nt(d_own, w_own) + nt(d_sib, w_sib)
    input_grad = give_back(d_input.astype(BF))
    joined_grad = scatter_rows(join(tn(x, d_own), tn(x, d_sib), c, hw))
    vec = [v.reshape(shards, -1) for v in (d_bias, d_gain_one, d_shift_one, d_gain_two, d_shift_two)]
    vec = lax.psum(lax.psum_scatter(jnp.concatenate(vec, axis=1), "shard", scatter_dimension=0, tiled=True), "seq")[0]
    vecs = [vec[a:b] for a, b in zip(cuts[:-1], cuts[1:])]
    return (
        result,
        input_grad,
        joined_grad[:, :width],
        joined_grad[:, width : 2 * width],
        joined_grad[:, 2 * width :],
        projection_grad,
        inner_grad,
        vecs[0],
        outer_grad,
        vecs[1],
        vecs[2],
        vecs[3],
        vecs[4],
    )


def solution(mesh):
    act = P("shard", "seq", None)
    mat = P("shard", None)
    vec = P("shard")
    return jax.shard_map(
        body,
        mesh=mesh,
        in_specs=(act, act, mat, mat, mat, mat, mat, vec, mat, vec, vec, vec, vec, mat, P("shard", None, None)),
        out_specs=(act, act, mat, mat, mat, mat, mat, vec, mat, vec, vec, vec, vec),
        check_vma=False,
    )
```

time: 2130 us -> 778 us (0.37)
  waiting for transfers between devices: 973 us -> 321 us
  matrix products: 720 us -> 108 us
  Pallas kernels: 0 us -> 140 us
  other arithmetic: 130 us -> 23.3 us
  local copies, waits for them, and re-layouts: 156 us -> 52.7 us
  starting transfers between devices: 33.5 us -> 7.86 us
    dot_general x72 -> x15, matrix products: 720 us -> 108 us  [the longest x5 40.5 us: nt(): lax.dot_general(a, b, (((1,), (1,)), ((), ())), preferred_element_type=F32)]
    reduce_scatter x6 -> x4, waiting for transfers between devices: 596 us -> 210 us  [scatter_rows(): lax.psum_scatter(grad.astype(BF), ('shard', 'seq'), scatter_dimension=0,...]
    all_gather x6 -> x4, waiting for transfers between devices: 269 us -> 110 us  [gather_rows(): return lax.all_gather(mine, ('shard', 'seq'), axis=0, tiled=True)]
    pallas_call x0 -> x2, Pallas kernels: none -> 140 us  [the longest x1 86.5 us: bwd_call(): pl.pallas_call(kern, name='attn_bwd', out_shape=jax.ShapeDtypeStruct((seq...]
    all_to_all x8 -> x0, waiting for transfers between devices: 100 us -> none  [the longest x2 67 us: micro_step(): lax.all_to_all(d_joined, 'seq', split_axis=0, concat_axis=2, tiled=True)]
    reduce_sum x22 -> x9, other arithmetic: 63.8 us -> 7.21 us  [the longest x1 4.43 us: body(): d_gain_two = jnp.sum(cot * n_two, axis=0)]
    slice x13 -> x6, local copies, waits for them, and re-layouts: 43.8 us -> 4.24 us  [the longest x1 2.05 us: body(): d_sib = swap(d_qkv[2 * local:], 1, groups)]
    all_gather x1 -> x5, blocking collectives: 26 us -> 59.2 us  [the longest x1 31 us: body(): lax.all_gather(small_local, 'shard', axis=0, tiled=False).astype(F32)]
  transfers between devices with their start and end apart: 21 -> 16, of which waited for: 20 -> 7; matrix products, arithmetic and copies ran while one was open for 6% -> 17% of each run, Pallas kernels for 0% -> 18%
where the time goes in v1:
time: 778 us; the launch traced here: 769 us
  waiting for transfers between devices  321 us (41%)
  Pallas kernels  140 us (18%)
  matrix products  108 us (14%)
  blocking collectives  101 us (13%)
  local copies, waits for them, and re-layouts  52.7 us (7%)
  other arithmetic  23.3 us (3%)
  between operations  15.1 us (2%)
  starting transfers between devices  7.86 us (1%)
    reduce_scatter x4, waiting for transfers between devices, scatter_rows(): lax.psum_scatter(grad.astype(BF), ('shard', 'seq'), scatter_dimension=0,...  210 us
    all_gather x4, waiting for transfers between devices, gather_rows(): return lax.all_gather(mine, ('shard', 'seq'), axis=0, tiled=True)  110 us
    pallas_call x1, Pallas kernels, bwd_call(): pl.pallas_call(kern, name='attn_bwd', out_shape=jax.ShapeDtypeStruct((seq...  86.5 us
    pallas_call x1, Pallas kernels, fwd_call(): pl.pallas_call(kern, name='attn_fwd', out_shape=(jax.ShapeDtypeStruct((se...  53.1 us
    dot_general x5, matrix products, nt(): lax.dot_general(a, b, (((1,), (1,)), ((), ())), preferred_element_type=F32)  40.5 us
    unnamed x1, blocking collectives  36.3 us
    dot_general x5, matrix products, nn(): lax.dot_general(a, b, (((1,), (0,)), ((), ())), preferred_element_type=F32)  34 us
    dot_general x5, matrix products, tn(): lax.dot_general(a, b, (((0,), (0,)), ((), ())), preferred_element_type=F32)  33.3 us
  transfers between devices with their start and end apart: 16, of which 7 were waited for; matrix products, arithmetic and copies ran while one was open for 17% of the time, Pallas kernels for 18%

profile of v1, /device:TPU:0, one launch (start us, length us, event | category | flops | bytes accessed | tf_op | source)
XLA Modules:
  0.0 768.7 jit_solution(10786707383173899302)
XLA Ops:
  24.9 49.8 %all-gather.7.cloned.1.call-done = bf16[768,2304]{1,0:T(8,128)(2,1)} async-done(((bf16[24,2304]{1,0:T(8,128)(2,1)}), bf16[768,2304]{1,0:T(8,128)(2,1)}) %all-gather.7.cloned.1.call-update) | async-done | bytes 3538960 | tf_op jit(solution)/shard_map/all_gather | solution.py:209
  74.8 4.5 copy.98
  89.0 4.8 convolution_convert_fusion.3.mine_ref
  95.1 53.1 %attn_fwd.1 = (bf16[2048,384]{1,0:T(8,128)(2,1)}, f32[4096,128]{1,0:T(8,128)}) custom-call(s32[32,32]{1,0:T(8,128)} %broadcast_add_fusion.idx_ref, s32[32]{0:T(128)} %and_select_fusion.cnt_ref, bf16[1024,1152]{1,0:T(8,128)(2,1)} %convolution_convert_fusion.3.mine_ref, bf16[1024,1152]{1,0:T(8,128)(2,1)} %copy-done.34, ...), custom_call_target="tpu_custom_call" | custom-call | flops 20000000000 | bytes 12000000 | tf_op jit(solution)/shard_map/attn_fwd/pallas_call | solution.py:80
  152.4 31.0 %all-gather.1 = bf16[8,1,768]{2,1,0:T(2,128)(2,1)S(1)} all-gather(bf16[1,1,768]{2,1,0:T(2,128)(2,1)S(1)} %reshape.572), channel_id=2, replica_groups=mesh['shard'=8,'seq'=4] {'shard'}, dimensions={0}, use_global_device_ids=true | all-gather | bytes 13824 | tf_op jit(solution)/shard_map/all_gather | solution.py:245
  192.6 5.3 all-gather.11.cloned.1.call-done
  197.9 10.6 %fusion.38 = f32[1024,3072]{1,0:T(8,128)} fusion(bf16[768,3072]{1,0:T(8,128)(2,1)} %all-gather.11.cloned.1.call-done, f32[1024,768]{0,1:T(8,128)S(1)} %get-tuple-element.95, f32[768]{0:T(1024)S(1)} %add.245, f32[768]{0:T(1024)S(1)} %mul.180, f32[1024]{0:T(1024)S(1)} %add_rsqrt_fusion.1, f32[1024]{0:T(1024)S(1)} %broadcast_multiply_fusion.5), kind=kOutput, calls=%fused_computation.144 | convolution fusion | flops 4835770368 | bytes 20461568 | tf_op jit(solution)/shard_map/dot_general | solution.py:16
  208.5 54.7 %all-gather.13.cloned.1.call-done = bf16[3072,768]{1,0:T(8,128)(2,1)} async-done(((bf16[96,768]{1,0:T(8,128)(2,1)}), bf16[3072,768]{1,0:T(8,128)(2,1)}) %all-gather.13.cloned.1.call-update) | async-done | bytes 4718608 | tf_op jit(solution)/shard_map/all_gather | solution.py:209
  263.2 11.1 %fusion.46 = (f32[1024]{0:T(1024)S(1)}, f32[1024,768]{0,1:T(8,128)S(1)}) fusion(bf16[3072,768]{1,0:T(8,128)(2,1)} %all-gather.13.cloned.1.call-done, f32[1024,3072]{1,0:T(8,128)} %fusion.38, f32[3072]{0:T(1024)S(1)} %add.248, f32[768]{0:T(1024)S(1)} %add.245, f32[768]{0:T(1024)S(1)} %mul.180, f32[1024]{0:T(1024)S(1)} %add_rsqrt_fusion.1, ...), kind=kOutput, calls=%fused_computation.148 | convolution fusion | flops 4868013056 | bytes 23623680 | tf_op jit(solution)/shard_map/dot_general | solution.py:16
  276.0 4.4 fusion.14
  280.5 19.8 %convert_reduce_fusion = (f32[3072]{0:T(1024)S(1)}, bf16[1024,3072]{1,0:T(8,128)(2,1)}) fusion(f32[1024,3072]{1,0:T(8,128)} %fusion.38, f32[3072]{0:T(1024)S(1)} %add.248, bf16[3072,768]{1,0:T(8,128)(2,1)} %all-gather.13.cloned.1.call-done, f32[1024]{0:T(1024)S(1)} %broadcast_multiply_fusion.2, f32[1024]{0:T(1024)S(1)} %add_rsqrt_fusion, ...), kind=kOutput, calls=%fused_computation.9 | convolution fusion | flops 4910478336 | bytes 28355584 | tf_op jit(solution)/shard_map/dot_general | solution.py:14
  300.2 11.3 %multiply_reduce_fusion = (f32[768]{0:T(1024)}, f32[1024]{0:T(1024)S(1)}, f32[1024]{0:T(1024)S(1)}, f32[768]{0:T(1024)S(1)}, f32[1024,768]{0,1:T(8,128)S(1)}) fusion(f32[1024,768]{0,1:T(8,128)S(1)} %get-tuple-element.95, f32[1024]{0:T(1024)S(1)} %add_rsqrt_fusion.1, f32[1024]{0:T(1024)S(1)} %broadcast_multiply_fusion.5, f32[768]{0:T(1024)S(1)} %mul.180, ...), kind=kOutput, calls=%fused_computation.27 | convolution fusion | flops 4848349184 | bytes 22065152 | tf_op jit(solution)/shard_map/dot_general | solution.py:14
  316.6 10.0 %convolution_convert_fusion.1 = bf16[768,3072]{1,0:T(8,128)(2,1)} fusion(bf16[1024,3072]{1,0:T(8,128)(2,1)} %get-tuple-element.132, f32[1024,768]{0,1:T(8,128)S(1)} %get-tuple-element.95, f32[768]{0:T(1024)S(1)} %add.245, f32[768]{0:T(1024)S(1)} %mul.180, f32[1024]{0:T(1024)S(1)} %add_rsqrt_fusion.1, f32[1024]{0:T(1024)S(1)} %broadcast_multiply_fusion.5), kind=kOutput, calls=%fused_computation.14 | convolution fusion | flops 4838129664 | bytes 14170112 | tf_op jit(solution)/shard_map/dot_general | solution.py:15
  335.3 13.8 %convolution_convert_fusion = bf16[3072,768]{1,0:T(8,128)(2,1)} fusion(f32[1024,768]{0,1:T(8,128)S(1)} %copy-done.3, f32[1024]{0:T(1024)S(1)} %broadcast_multiply_fusion.2, f32[1024]{0:T(1024)S(1)} %broadcast_multiply_fusion.3, f32[768]{0:T(1024)S(1)} %mul.194, f32[1024]{0:T(1024)S(1)} %add_rsqrt_fusion, f32[1024]{0:T(1024)S(1)} %broadcast_multiply_fusion.4, ...), kind=kOutput, calls=%fused_computation.13 | convolution fusion | flops 4875091968 | bytes 22051840 | tf_op jit(solution)/shard_map/dot_general | solution.py:15
  351.5 86.5 %attn_bwd.1 = bf16[2048,1152]{1,0:T(8,128)(2,1)} custom-call(s32[32,32]{1,0:T(8,128)} %broadcast_add_fusion.idx_ref, s32[32]{0:T(128)} %and_select_fusion.cnt_ref, bf16[1024,1152]{1,0:T(8,128)(2,1)} %convolution_convert_fusion.3.mine_ref, bf16[1024,1152]{1,0:T(8,128)(2,1)} %copy-done.34, bf16[1024,384]{1,0:T(8,128)(2,1)} %bitcast.85, ...), custom_call_target="tpu_custom_call" | custom-call | flops 49999998976 | bytes 18000000 | tf_op jit(solution)/shard_map/attn_bwd/pallas_call | solution.py:153
  467.5 36.3 %all-reduce.1 = f32[8,768]{1,0:T(8,128)S(1)} all-reduce(f32[8,768]{1,0:T(8,128)S(1)} %concatenate.64), channel_id=6, replica_groups=mesh['shard'=8,'seq'=4] {'shard'}, use_global_device_ids=true, to_apply=%region_26.27.clone | all-reduce | flops 6144 | bytes 49152
  504.5 5.9 psum.7
  515.8 5.7 all_gather.37
  525.5 8.0 %reduce-scatter.9.cloned.1.call-done = bf16[24,3072]{1,0:T(8,128)(2,1)} async-done(((bf16[768,3072]{1,0:T(8,128)(2,1)}), bf16[24,3072]{1,0:T(8,128)(2,1)}) %reduce-scatter.9.cloned.1.call-update) | async-done | bytes 147472 | tf_op jit(solution)/shard_map/reduce_scatter | solution.py:213
  533.5 7.8 %all_gather.38 = bf16[96,3072]{1,0:T(8,128)(2,1)S(1)} all-gather(bf16[24,3072]{1,0:T(8,128)(2,1)} %reduce-scatter.9.cloned.1.call-done), channel_id=1, replica_groups=mesh['shard'=8,'seq'=4] {'seq'}, dimensions={0}, use_global_device_ids=true | all-gather | bytes 737280 | tf_op jit(solution)/shard_map/all_gather | solution.py:214
  542.4 103.3 %reduce-scatter.11.cloned.1.call-done = bf16[96,768]{1,0:T(8,128)(2,1)} async-done(((bf16[3072,768]{1,0:T(8,128)(2,1)}), bf16[96,768]{1,0:T(8,128)(2,1)}) %reduce-scatter.11.cloned.1.call-update) | async-done | bytes 147472 | tf_op jit(solution)/shard_map/reduce_scatter | solution.py:213
  645.7 7.7 %all_gather.39 = bf16[384,768]{1,0:T(8,128)(2,1)S(1)} all-gather(bf16[96,768]{1,0:T(8,128)(2,1)} %reduce-scatter.11.cloned.1.call-done), channel_id=1, replica_groups=mesh['shard'=8,'seq'=4] {'seq'}, dimensions={0}, use_global_device_ids=true | all-gather | bytes 737280 | tf_op jit(solution)/shard_map/all_gather | solution.py:214
  654.5 99.0 %reduce-scatter.13.cloned.1.call-done = bf16[24,2304]{1,0:T(8,128)(2,1)} async-done(((bf16[768,2304]{1,0:T(8,128)(2,1)}), bf16[24,2304]{1,0:T(8,128)(2,1)}) %reduce-scatter.13.cloned.1.call-update) | async-done | bytes 110608 | tf_op jit(solution)/shard_map/reduce_scatter | solution.py:213
  753.6 7.0 all_gather.36
  (210 shorter events, 102.0 us)
Async XLA Ops:
  7.2 67.6 %all-gather.7.cloned.1.call-start = ((), (), s32[]{:S(2)}) async-start(), calls=%async_computation.4 | async-start | bytes 3649536 | tf_op jit(solution)/shard_map/all_gather | solution.py:209
  8.8 179.6 %all-gather.9.cloned.1.call-start = ((), (), s32[]{:S(2)}) async-start(), calls=%async_computation.5 | async-start | bytes 1216512 | tf_op jit(solution)/shard_map/all_gather | solution.py:209
  10.3 187.7 %all-gather.11.cloned.1.call-start = ((), (), s32[]{:S(2)}) async-start(), calls=%async_computation.6 | async-start | bytes 4866048 | tf_op jit(solution)/shard_map/all_gather | solution.py:209
  11.0 252.2 %all-gather.13.cloned.1.call-start = ((), (), s32[]{:S(2)}) async-start(), calls=%async_computation.7 | async-start | bytes 4866048 | tf_op jit(solution)/shard_map/all_gather | solution.py:209
  11.1 9.4 %copy-start.33 = (s32[2,3]{1,0:T(2,128)S(1)}, s32[2,3]{1,0:T(2,128)}, u32[]{:S(2)}) copy-start(s32[2,3]{1,0:T(2,128)} %param.28) | copy-start | bytes 76
  11.1 9.4 %copy-start.26 = (s32[2,32,3]{1,0,2:T(2,128)S(1)}, s32[2,32,3]{1,0,2:T(2,128)}, u32[]{:S(2)}) copy-start(s32[2,32,3]{1,0,2:T(2,128)} %param.29) | copy-start | bytes 2308
  15.5 64.1 %collective-permute-start = (bf16[512,768]{0,1:T(8,128)(2,1)}, bf16[512,768]{0,1:T(8,128)(2,1)}, u32[]{:S(2)}, u32[]{:S(2)}) collective-permute-start(bf16[512,768]{0,1:T(8,128)(2,1)} %bitcast.1), channel_id=1, source_target_pairs={{0,2},{1,3},{2,0},{3,1},{4,6},{5,7},{6,4},{7,5},{8,10},{9,11},{10,... | collective-permute-start | bytes 2359304 | tf_op jit(solution)/shard_map/ppermute | solution.py:189
  20.1 495.7 %reduce-scatter.7.cloned.1.call-start = ((), (), s32[]{:S(2)}) async-start(), calls=%async_computation.8 | async-start | bytes 1216512 | tf_op jit(solution)/shard_map/reduce_scatter | solution.py:213
  79.6 9.4 %copy-start.13 = (bf16[768,3,1,384]{0,3,2,1:T(8,128)(2,1)}, bf16[768,3,1,384]{0,3,2,1:T(8,128)(2,1)S(1)}, u32[]{:S(2)}) copy-start(bf16[768,3,1,384]{0,3,2,1:T(8,128)(2,1)S(1)} %get-tuple-element.101) | copy-start | bytes 5308420
  80.4 7.4 copy-start.21
  84.2 9.5 %collective-permute-start.1 = (bf16[1024,1152]{1,0:T(8,128)(2,1)S(1)}, bf16[1024,1152]{1,0:T(8,128)(2,1)S(1)}, u32[]{:S(2)}, u32[]{:S(2)}) collective-permute-start(bf16[1024,1152]{1,0:T(8,128)(2,1)S(1)} %convolution_convert_fusion.2), channel_id=1, source_target_pairs={{0,1},{1,0},{2,3},{3,2},{4,5},{5,4},{6,7},{7,6},{8,9},{9,8},{10,11... | collective-permute-start | bytes 7077896 | tf_op jit(solution)/shard_map/ppermute | solution.py:189
  148.2 35.5 %copy-start.9 = (bf16[1,512,768]{2,1,0:T(8,128)(2,1)S(1)}, bf16[1,512,768]{2,1,0:T(8,128)(2,1)}, u32[]{:S(2)}) copy-start(bf16[1,512,768]{2,1,0:T(8,128)(2,1)} %get-tuple-element.107) | copy-start | bytes 2359300
  149.9 35.2 %collective-permute-start.2 = (bf16[1024,384]{1,0:T(8,128)(2,1)S(1)}, bf16[1024,384]{1,0:T(8,128)(2,1)}, u32[]{:S(2)}, u32[]{:S(2)}) collective-permute-start(bf16[1024,384]{1,0:T(8,128)(2,1)S(1)} %get-tuple-element.112), channel_id=1, source_target_pairs={{0,1},{1,0},{2,3},{3,2},{4,5},{5,4},{6,7},{7,6},{8,9},{9,8},{10,11... | collective-permute-start | bytes 2359304 | tf_op jit(solution)/shard_map/ppermute | solution.py:189
  151.4 123.3 %collective-permute-start.4 = (bf16[512,768]{0,1:T(8,128)(2,1)}, bf16[512,768]{0,1:T(8,128)(2,1)}, u32[]{:S(2)}, u32[]{:S(2)}) collective-permute-start(bf16[512,768]{0,1:T(8,128)(2,1)} %bitcast.18), channel_id=1, source_target_pairs={{0,2},{1,3},{2,0},{3,1},{4,6},{5,7},{6,4},{7,5},{8,10},{9,11},{10,... | collective-permute-start | bytes 2359304 | tf_op jit(solution)/shard_map/ppermute | solution.py:189
  274.3 25.9 %copy-start.2 = (f32[1024,768]{0,1:T(8,128)}, f32[1024,768]{0,1:T(8,128)S(1)}, u32[]{:S(2)}) copy-start(f32[1024,768]{0,1:T(8,128)S(1)} %get-tuple-element.129) | copy-start | bytes 9437188
  316.6 216.9 %reduce-scatter.9.cloned.1.call-start = ((), (), s32[]{:S(2)}) async-start(), calls=%async_computation.9 | async-start | bytes 4866048 | tf_op jit(solution)/shard_map/reduce_scatter | solution.py:213
  326.6 319.1 %reduce-scatter.11.cloned.1.call-start = ((), (), s32[]{:S(2)}) async-start(), calls=%async_computation.10 | async-start | bytes 4866048 | tf_op jit(solution)/shard_map/reduce_scatter | solution.py:213
  335.0 16.5 %collective-permute-start.5 = (bf16[1024,384]{1,0:T(8,128)(2,1)}, bf16[1024,384]{1,0:T(8,128)(2,1)}, u32[]{:S(2)}, u32[]{:S(2)}) collective-permute-start(bf16[1024,384]{1,0:T(8,128)(2,1)} %bitcast.84), channel_id=1, source_target_pairs={{0,1},{1,0},{2,3},{3,2},{4,5},{5,4},{6,7},{7,6},{8,9},{9,8},{10,11... | collective-permute-start | bytes 2359304 | tf_op jit(solution)/shard_map/ppermute | solution.py:189
  351.5 402.1 %reduce-scatter.13.cloned.1.call-start = ((), (), s32[]{:S(2)}) async-start(), calls=%async_computation.11 | async-start | bytes 3649536 | tf_op jit(solution)/shard_map/reduce_scatter | solution.py:213
  351.5 88.9 %copy-start.18 = (bf16[1,512,768]{1,2,0:T(8,128)(2,1)S(1)}, bf16[1,512,768]{1,2,0:T(8,128)(2,1)}, u32[]{:S(2)}) copy-start(bf16[1,512,768]{1,2,0:T(8,128)(2,1)} %copy.96) | copy-start | bytes 2359300
  440.1 5.0 collective-permute-start.6
  456.4 55.3 %collective-permute-start.3 = (bf16[512,768]{0,1:T(8,128)(2,1)}, bf16[512,768]{0,1:T(8,128)(2,1)S(1)}, u32[]{:S(2)}, u32[]{:S(2)}) collective-permute-start(bf16[512,768]{0,1:T(8,128)(2,1)} %get-tuple-element.110), channel_id=1, source_target_pairs={{0,2},{1,3},{2,0},{3,1},{4,6},{5,7},{6,4},{7,5},{8,10},{9,11},{10,... | collective-permute-start | bytes 2359304 | tf_op jit(solution)/shard_map/ppermute | solution.py:189
  464.6 57.5 %collective-permute-start.7 = (bf16[512,768]{0,1:T(8,128)(2,1)}, bf16[512,768]{0,1:T(8,128)(2,1)}, u32[]{:S(2)}, u32[]{:S(2)}) collective-permute-start(bf16[512,768]{0,1:T(8,128)(2,1)} %get-tuple-element.104), channel_id=1, source_target_pairs={{0,2},{1,3},{2,0},{3,1},{4,6},{5,7},{6,4},{7,5},{8,10},{9,11},{10,... | collective-permute-start | bytes 2359304 | tf_op jit(solution)/shard_map/ppermute | solution.py:189
  533.5 228.0 %copy-start.1 = (bf16[96,3072]{1,0:T(8,128)(2,1)S(1)}, bf16[96,3072]{1,0:T(8,128)(2,1)}, u32[]{:S(2)}) copy-start(bf16[96,3072]{1,0:T(8,128)(2,1)} %param.21) | copy-start | bytes 1769476
  (30 other events, 99.2 us)
Sparse Core Ops, SparseCore 0:
  11.5 63.2 all-gather.6
  78.3 52.8 all-gather.8
  134.6 63.2 all-gather.10
  201.2 61.8 all-gather.12
  316.7 95.4 reduce-scatter.6
  417.5 115.9 reduce-scatter.8
  539.0 106.6 reduce-scatter.10
  651.1 102.3 reduce-scatter.12

commit v2 on v1

--- a/solution.py
+++ b/solution.py
@@ -15,20 +15,19 @@
 def tn(a,b): return lax.dot_general(a,b,(((0,),(0,)),((),())),preferred_element_type=F32)
 def nn(a,b): return lax.dot_general(a,b,(((1,),(0,)),((),())),preferred_element_type=F32)
 
-def fwd_call(mine, recv, qmask, kmask, idx, cnt):
-    half=mine.shape[0]; seq=2*half; nb=seq//BLK; width=mine.shape[1]//3; pairs=width//PAIR
+def fwd_call(qkv, qmask, kmask, idx, cnt):
+    seq=qkv.shape[0]; half=seq//2; nb=seq//BLK; width=qkv.shape[1]//3; pairs=width//PAIR
     rows=2*BLK; gk=GRP*BLK; maxg=nb//GRP
-    def kern(idx_ref,cnt_ref,mine_ref,recv_ref,qm_ref,km_ref,out_ref,log_ref,kx,vx,s_scr,mx,acc,ls):
+    def kern(idx_ref,cnt_ref,qkv_ref,qm_ref,km_ref,om_ref,os_ref,log_ref,kx,vx,s_scr,mx,acc,ls):
         lane=lax.broadcasted_iota(jnp.int32,(BLK,PAIR),1)
         low=lane<BLK
         for p in range(pairs):
-            for t,src in ((0,mine_ref),(1,recv_ref)):
-                kx[p,t*half:(t+1)*half,:PAIR]=src[:,width+p*PAIR:width+(p+1)*PAIR]
-                vx[p,t*half:(t+1)*half,:]=src[:,2*width+p*PAIR:2*width+(p+1)*PAIR]
+            kx[p,:seq,:PAIR]=qkv_ref[:,width+p*PAIR:width+(p+1)*PAIR]
+            vx[p,:seq,:]=qkv_ref[:,2*width+p*PAIR:2*width+(p+1)*PAIR]
             kx[p,seq:seq+BLK,:PAIR]=jnp.zeros((BLK,PAIR),BF)
             vx[p,seq:seq+BLK,:]=jnp.zeros((BLK,PAIR),BF)
             kx[p,:,PAIR:]=km_ref[...]
-        def half_loop(src_ref,base):
+        def half_loop(out_ref,base):
             def qblock(b,_):
                 i=base+b
                 n=cnt_ref[i]
@@ -36,7 +35,7 @@
                 qm=qm_ref[pl.ds(pl.multiple_of(i*BLK,BLK),BLK),:]
                 qs=[]
                 for p in range(pairs):
-                    q=src_ref[pl.ds(qrow,BLK),p*PAIR:(p+1)*PAIR]*jnp.asarray(0.125,BF)
+                    q=qkv_ref[pl.ds(pl.multiple_of(i*BLK,BLK),BLK),p*PAIR:(p+1)*PAIR]*jnp.asarray(0.125,BF)
                     z=jnp.zeros_like(q)
                     stk=jnp.concatenate([jnp.where(low,q,z),jnp.where(low,z,q)],axis=0)
                     qs.append(jnp.concatenate([stk,jnp.concatenate([qm,qm],axis=0)],axis=1))
@@ -68,39 +67,38 @@
                     l=jnp.sum(ls[p],axis=1,keepdims=True)
                     o=acc[p]*(1.0/l)
                     o=jnp.where(low,o[:BLK],o[BLK:])
-                    out_ref[pl.ds(pl.multiple_of(i*BLK,BLK),BLK),p*PAIR:(p+1)*PAIR]=o.astype(BF)
+                    out_ref[pl.ds(qrow,BLK),p*PAIR:(p+1)*PAIR]=o.astype(BF)
                     logs=jnp.where(lanes==p,ms[p]+jnp.log(l),logs)
                 log_ref[pl.ds(pl.multiple_of(i*rows,rows),rows),:]=logs
                 return 0
             lax.fori_loop(0,nb//2,qblock,0)
-        half_loop(mine_ref,0)
-        half_loop(recv_ref,nb//2)
+        half_loop(om_ref,0)
+        half_loop(os_ref,nb//2)
     v=pl.BlockSpec(memory_space=pltpu.VMEM)
     s=pl.BlockSpec(memory_space=pltpu.SMEM)
     return pl.pallas_call(kern,name="attn_fwd",
-        out_shape=(jax.ShapeDtypeStruct((seq,width),BF),jax.ShapeDtypeStruct((nb*rows,PAIR),F32)),
-        in_specs=[s,s,v,v,v,v],out_specs=(v,v),
+        out_shape=(jax.ShapeDtypeStruct((half,width),BF),jax.ShapeDtypeStruct((half,width),BF),jax.ShapeDtypeStruct((nb*rows,PAIR),F32)),
+        in_specs=[s,s,v,v,v],out_specs=(v,v,v),
         scratch_shapes=[pltpu.VMEM((pairs,seq+BLK,2*PAIR),BF),pltpu.VMEM((pairs,seq+BLK,PAIR),BF),
             pltpu.VMEM((maxg,pairs,rows,gk),F32),pltpu.VMEM((pairs,rows,PAIR),F32),pltpu.VMEM((pairs,rows,PAIR),F32),pltpu.VMEM((pairs,rows,PAIR),F32)],
         cost_estimate=pl.CostEstimate(flops=20_000_000_000,transcendentals=12_000_000,bytes_accessed=12_000_000),
-    )(idx,cnt,mine,recv,qmask,kmask)
-
-def bwd_call(mine, recv, dmine, drecv, out, logs, qmask, kmask, idx, cnt):
-    half=mine.shape[0]; seq=2*half; nb=seq//BLK; width=mine.shape[1]//3; pairs=width//PAIR
+    )(idx,cnt,qkv,qmask,kmask)
+
+def bwd_call(qkv, dmine, drecv, omine, orecv, logs, qmask, kmask, idx, cnt):
+    seq=qkv.shape[0]; half=seq//2; nb=seq//BLK; width=qkv.shape[1]//3; pairs=width//PAIR
     rows=2*BLK; gk=GRP*BLK
-    def kern(idx_ref,cnt_ref,mine_ref,recv_ref,dm_ref,dr_ref,o_ref,log_ref,qm_ref,km_ref,g_ref,kx,vx,dk,dv,dq):
+    def kern(idx_ref,cnt_ref,qkv_ref,dm_ref,dr_ref,om_ref,or_ref,log_ref,qm_ref,km_ref,g_ref,kx,vx,dk,dv,dq):
         lane=lax.broadcasted_iota(jnp.int32,(BLK,PAIR),1)
         low=lane<BLK
         for p in range(pairs):
-            for t,src in ((0,mine_ref),(1,recv_ref)):
-                kx[p,t*half:(t+1)*half,:PAIR]=src[:,width+p*PAIR:width+(p+1)*PAIR]
-                vx[p,t*half:(t+1)*half,:]=src[:,2*width+p*PAIR:2*width+(p+1)*PAIR]
+            kx[p,:seq,:PAIR]=qkv_ref[:,width+p*PAIR:width+(p+1)*PAIR]
+            vx[p,:seq,:]=qkv_ref[:,2*width+p*PAIR:2*width+(p+1)*PAIR]
             kx[p,seq:seq+BLK,:PAIR]=jnp.zeros((BLK,PAIR),BF)
             vx[p,seq:seq+BLK,:]=jnp.zeros((BLK,PAIR),BF)
             kx[p,:,PAIR:]=km_ref[...]
             dk[p]=jnp.zeros((seq+BLK,PAIR),F32)
             dv[p]=jnp.zeros((seq+BLK,PAIR),F32)
-        def half_loop(src_ref,dsrc_ref,base):
+        def half_loop(o_ref,dsrc_ref,base):
             def qblock(b,_):
                 i=base+b
                 n=cnt_ref[i]
@@ -110,13 +108,13 @@
                 logs=log_ref[pl.ds(pl.multiple_of(i*rows,rows),rows),:]
                 qs=[];ds_=[];ls_=[];dl=[]
                 for p in range(pairs):
-                    q=src_ref[pl.ds(qrow,BLK),p*PAIR:(p+1)*PAIR]*jnp.asarray(0.125,BF)
+                    q=qkv_ref[pl.ds(pl.multiple_of(i*BLK,BLK),BLK),p*PAIR:(p+1)*PAIR]*jnp.asarray(0.125,BF)
                     z=jnp.zeros_like(q)
                     stk=jnp.concatenate([jnp.where(low,q,z),jnp.where(low,z,q)],axis=0)
                     qs.append(jnp.concatenate([stk,jnp.concatenate([qm,qm],axis=0)],axis=1))
                     d=dsrc_ref[pl.ds(qrow,BLK),p*PAIR:(p+1)*PAIR]
                     ds_.append(jnp.concatenate([jnp.where(low,d,z),jnp.where(low,z,d)],axis=0))
-                    prod=d.astype(F32)*o_ref[pl.ds(irow,BLK),p*PAIR:(p+1)*PAIR].astype(F32)
+                    prod=d.astype(F32)*o_ref[pl.ds(qrow,BLK),p*PAIR:(p+1)*PAIR].astype(F32)
                     zf=jnp.zeros_like(prod)
                     dl.append(jnp.sum(jnp.concatenate([jnp.where(low,prod,zf),jnp.where(low,zf,prod)],axis=0),axis=1,keepdims=True))
                     ls_.append(logs[:,p:p+1])
@@ -143,8 +141,8 @@
                     g_ref[pl.ds(irow,BLK),p*PAIR:(p+1)*PAIR]=(jnp.where(low,g[:BLK],g[BLK:])*0.125).astype(BF)
                 return 0
             lax.fori_loop(0,nb//2,qblock,0)
-        half_loop(mine_ref,dm_ref,0)
-        half_loop(recv_ref,dr_ref,nb//2)
+        half_loop(om_ref,dm_ref,0)
+        half_loop(or_ref,dr_ref,nb//2)
         for p in range(pairs):
             g_ref[:,width+p*PAIR:width+(p+1)*PAIR]=dk[p,:seq].astype(BF)
             g_ref[:,2*width+p*PAIR:2*width+(p+1)*PAIR]=dv[p,:seq].astype(BF)
@@ -156,7 +154,7 @@
         scratch_shapes=[pltpu.VMEM((pairs,seq+BLK,2*PAIR),BF),pltpu.VMEM((pairs,seq+BLK,PAIR),BF),
             pltpu.VMEM((pairs,seq+BLK,PAIR),F32),pltpu.VMEM((pairs,seq+BLK,PAIR),F32),pltpu.VMEM((pairs,rows,PAIR),F32)],
         cost_estimate=pl.CostEstimate(flops=50_000_000_000,transcendentals=12_000_000,bytes_accessed=18_000_000),
-    )(idx,cnt,mine,recv,dmine,drecv,out,logs,qmask,kmask)
+    )(idx,cnt,qkv,dmine,drecv,omine,orecv,logs,qmask,kmask)
 
 def tables(starts, chosen, orig, seq):
     nb=orig.shape[0]
@@ -189,11 +187,60 @@
     return lax.ppermute(value, "seq", [(s, s ^ flip) for s in range(groups)])
 
 
-def halves(full, c, width):
-    parts = full.reshape(full.shape[0], -1, 2, width)
-    own = lax.dynamic_index_in_dim(parts, c, 2, keepdims=False)
-    other = lax.dynamic_index_in_dim(parts, 1 - c, 2, keepdims=False)
-    return own.reshape(full.shape[0], -1), other.reshape(full.shape[0], -1)
+def cross(value, bit, shards):
+    return lax.ppermute(value, "shard", [(i, i ^ (1 << bit)) for i in range(shards)])
+
+
+def staged(rows, shards):
+    return rows % 16 == 0 and shards & (shards - 1) == 0
+
+
+def arrange(pieces, place):
+    rows, width = pieces[0].shape
+    count = len(pieces)
+
+    def kern(at_ref, *refs):
+        for d in range(count):
+            row = pl.multiple_of((at_ref[0] ^ d) * rows, 16)
+            refs[count][pl.ds(row, rows), :] = refs[d][...]
+
+    vmem = pl.BlockSpec(memory_space=pltpu.VMEM)
+    return pl.pallas_call(
+        kern,
+        name="arrange",
+        out_shape=jax.ShapeDtypeStruct((count * rows, width), pieces[0].dtype),
+        in_specs=[pl.BlockSpec(memory_space=pltpu.SMEM)] + [vmem] * count,
+        out_specs=vmem,
+    )(place.reshape(1), *pieces)
+
+
+def gather_rows(local, place, shards):
+    have = {0: local}
+    for bit in reversed(range(shards.bit_length() - 1)):
+        for d in list(have):
+            have[d | (1 << bit)] = cross(have[d], bit, shards)
+    return arrange([have[d] for d in range(shards)], place)
+
+
+def sum_rows(grad, place, y, order, shards, groups):
+    total, width = grad.shape
+    rows = total // shards
+    if not staged(rows, shards):
+        share = lax.psum_scatter(grad, "shard", scatter_dimension=0, tiled=True)
+        return share + swap(share, 2, groups)
+    bits = shards.bit_length() - 1
+    left = list(reversed(range(bits))) + ["y"]
+    value = grad.reshape([2] * (bits + 1) + [rows // 2, width])
+    for step in order:
+        axis = left.index(step)
+        mine = y if step == "y" else (place >> step) & 1
+        send = lax.dynamic_index_in_dim(value, 1 - mine, axis, keepdims=False)
+        keep = lax.dynamic_index_in_dim(value, mine, axis, keepdims=False)
+        got = swap(send, 2, groups) if step == "y" else cross(send, step, shards)
+        value = (keep.astype(F32) + got.astype(F32)).astype(BF)
+        left.pop(axis)
+    other = swap(value, 2, groups)
+    return jnp.where(y == 0, jnp.concatenate([value, other]), jnp.concatenate([other, value]))
 
 
 def join(own, other, c, width):
@@ -203,15 +250,9 @@
     return both.reshape(own.shape[0], -1)
 
 
-def gather_rows(local, s, groups):
-    part = local.shape[0] // groups
-    mine = lax.dynamic_slice_in_dim(local, s * part, part, 0)
-    return lax.all_gather(mine, ("shard", "seq"), axis=0, tiled=True)
-
-
-def scatter_rows(grad):
-    share = lax.psum_scatter(grad.astype(BF), ("shard", "seq"), scatter_dimension=0, tiled=True)
-    return lax.all_gather(share, "seq", axis=0, tiled=True).astype(F32)
+def take_half(full, c, width):
+    parts = full.reshape(full.shape[0], -1, 2, width)
+    return lax.dynamic_index_in_dim(parts, c, 2, keepdims=False).reshape(full.shape[0], -1)
 
 
 def body(tokens, cotangent, query_weight, key_weight, value_weight, output_weight, inner_weight,
@@ -222,36 +263,60 @@
     assert rows == 2 and groups == 4
     seq = local * groups
     s = lax.axis_index("seq")
+    place = lax.axis_index("shard")
     c = s % 2
     y = s // 2
-    flip = 2
     hw = (H // 2) * HD
+    wrows = query_weight.shape[0]
+    frows = outer_weight.shape[0]
+    manual = staged(wrows // 2, shards) and staged(frows // 2, shards)
 
     def bring(pair):
         own = lax.dynamic_index_in_dim(pair, y, 0, keepdims=False)
-        away = swap(lax.dynamic_index_in_dim(pair, 1 - y, 0, keepdims=False), flip, groups)
-        return jnp.concatenate([own, away], axis=0)
+        return own, swap(lax.dynamic_index_in_dim(pair, 1 - y, 0, keepdims=False), 2, groups)
 
     def give_back(value):
+        away = swap(value[local:], 2, groups)
         own = value[:local]
-        away = swap(value[local:], flip, groups)
         return jnp.where(y == 0, jnp.stack([own, away]), jnp.stack([away, own]))
 
-    x = bring(tokens)
-    cot = bring(cotangent).astype(F32)
-    joined_local = jnp.concatenate([query_weight, key_weight, value_weight], axis=1)
-    joined = gather_rows(joined_local, s, groups)
+    def whole(part):
+        if manual:
+            return gather_rows(part, place, shards)
+        return lax.all_gather(part, "shard", axis=0, tiled=True)
+
+    x_near, x_far = bring(tokens)
+    x_near_sib = swap(x_near, 1, groups)
+    x_far_sib = swap(x_far, 1, groups)
+    x_all = jnp.concatenate([x_near, x_far, x_near_sib, x_far_sib], axis=0)
+    x = jnp.concatenate([x_near, x_far], axis=0)
+    w_qkv = whole(take_half(jnp.concatenate([query_weight, key_weight, value_weight], axis=1), c, hw))
     small_local = jnp.concatenate([inner_bias, first_gain, first_shift, second_gain, second_shift])
-    small = lax.all_gather(small_local, "shard", axis=0, tiled=False).astype(F32)
-    output_full = gather_rows(output_weight, s, groups)
-    inner_full = gather_rows(inner_weight, s, groups)
-    outer_full = gather_rows(outer_weight, s, groups)
+    out_half = take_half(output_weight, c, width // 2)
+    if manual:
+        extra = jnp.pad(small_local, (0, 16 * (width // 2) - small_local.shape[0])).reshape(16, width // 2)
+        gathered = whole(jnp.concatenate([out_half, extra], axis=0)).reshape(shards, wrows + 16, width // 2)
+        out_own = gathered[:, :wrows].reshape(width, width // 2)
+        small = gathered[:, wrows:].reshape(shards, -1)[:, : small_local.shape[0]]
+    else:
+        out_own = whole(out_half)
+        small = lax.all_gather(small_local, "shard", axis=0, tiled=False)
+    out_full = join(out_own, swap(out_own, 1, groups), c, width // 2)
+    in_own = whole(take_half(inner_weight, c, frows // 2))
+    in_sib = swap(in_own, 1, groups)
+    back_own = whole(lax.dynamic_slice_in_dim(outer_weight, c * (frows // 2), frows // 2, 0))
+    back_sib = swap(back_own, 1, groups)
+    cot_near, cot_far = bring(cotangent)
+    cot = jnp.concatenate([cot_near, cot_far], axis=0).astype(F32)
+    small = small.astype(F32)
     cuts = [0]
     for item in (inner_bias, first_gain, first_shift, second_gain, second_shift):
         cuts.append(cuts[-1] + item.shape[0])
     bias, gain_one, shift_one, gain_two, shift_two = [
         small[:, a:b].reshape(-1) for a, b in zip(cuts[:-1], cuts[1:])
     ]
+    bias_own = take_half(bias[None], c, frows // 2)
+    bias_sib = take_half(bias[None], 1 - c, frows // 2)
 
     nb = seq // BLK
     per = nb // groups
@@ -262,27 +327,29 @@
     chosen = jnp.sum(jnp.where((orig[:, None] == jnp.arange(nb)[None, :])[:, :, None], chosen[None], 0), axis=1)
     idx, cnt, qmask, kmask = tables(starts, chosen, orig, seq)
 
-    w_own, w_sib = halves(joined, c, hw)
-    sib_qkv = nn(x, w_sib).astype(BF)
-    recv_qkv = swap(sib_qkv, 1, groups)
-    own_qkv = nn(x, w_own).astype(BF)
-    context_all, logs = fwd_call(own_qkv, recv_qkv, qmask, kmask, idx, cnt)
-    ctx_own = context_all[: 2 * local]
-    ctx_sib = swap(context_all[2 * local :], 1, groups)
+    qkv = nn(x_all, w_qkv).astype(BF)
+    ctx_own, ctx_give, logs = fwd_call(qkv, qmask, kmask, idx, cnt)
+    ctx_sib = swap(ctx_give, 1, groups)
     context = join(ctx_own, ctx_sib, c, hw)
-    attended = nn(context, output_full)
+    attended = nn(context, out_full)
     res_one = x.astype(F32) + attended
     cen = res_one - jnp.mean(res_one, axis=-1, keepdims=True)
     rstd_one = lax.rsqrt(jnp.mean(cen * cen, axis=-1, keepdims=True) + EPS)
     n_one = cen * rstd_one
     first = n_one * gain_one + shift_one
     first_low = first.astype(BF)
-    inner = nn(first_low, inner_full) + bias
     root = 0.7978845608028654
-    tanh = jnp.tanh(root * (inner + 0.044715 * inner * inner * inner))
-    active = (0.5 * inner * (1.0 + tanh)).astype(BF)
-    slope = 0.5 * (1.0 + tanh) + 0.5 * inner * (1.0 - tanh * tanh) * root * (1.0 + 3 * 0.044715 * inner * inner)
-    outer = nn(active, outer_full)
+
+    def hidden(weight, bias_half):
+        inner = nn(first_low, weight) + bias_half
+        tanh = jnp.tanh(root * (inner + 0.044715 * inner * inner * inner))
+        active = (0.5 * inner * (1.0 + tanh)).astype(BF)
+        slope = 0.5 * (1.0 + tanh) + 0.5 * inner * (1.0 - tanh * tanh) * root * (1.0 + 3 * 0.044715 * inner * inner)
+        return active, slope
+
+    act_own, slope_own = hidden(in_own, bias_own)
+    act_sib, slope_sib = hidden(in_sib, bias_sib)
+    outer = nn(act_own, back_own) + nn(act_sib, back_sib)
     res_two = first + outer
     cen2 = res_two - jnp.mean(res_two, axis=-1, keepdims=True)
     rstd_two = lax.rsqrt(jnp.mean(cen2 * cen2, axis=-1, keepdims=True) + EPS)
@@ -293,36 +360,60 @@
     d_gain_two = jnp.sum(cot * n_two, axis=0)
     d_shift_two = jnp.sum(cot, axis=0)
     d_outer = d_second.astype(BF)
-    outer_grad = scatter_rows(tn(active, d_outer))
-    d_inner = (nt(d_outer, outer_full) * slope).astype(BF)
-    d_bias = jnp.sum(d_inner.astype(F32), axis=0)
-    inner_grad = scatter_rows(tn(first_low, d_inner))
-    d_first = d_second + nt(d_inner, inner_full)
+
+    def core_sum(own, give):
+        return (own + swap(give.astype(BF), 1, groups).astype(F32)).astype(BF)
+
+    top = shards.bit_length() - 1
+    zs = list(range(1, top))
+    back_grad = core_sum(tn(act_own, d_outer), tn(act_sib, d_outer))
+    back_grad = sum_rows(back_grad, place, y, ["y", 0] + zs, shards, groups)
+    di_own = (nt(d_outer, back_own) * slope_own).astype(BF)
+    di_sib = (nt(d_outer, back_sib) * slope_sib).astype(BF)
+    in_grad = core_sum(tn(first_low, di_own), tn(first_low, di_sib))
+    in_grad = sum_rows(in_grad, place, y, [0] + zs + ["y"], shards, groups)
+    d_first = d_second + nt(di_own, in_own) + nt(di_sib, in_sib)
     d_gain_one = jnp.sum(d_first * n_one, axis=0)
     d_shift_one = jnp.sum(d_first, axis=0)
     k_one = d_first * gain_one
     d_res = (k_one - jnp.mean(k_one, -1, keepdims=True) - n_one * jnp.mean(k_one * n_one, -1, keepdims=True)) * rstd_one
     d_attended = d_res.astype(BF)
-    projection_grad = scatter_rows(tn(context, d_attended))
-    d_context = nt(d_attended, output_full).astype(BF)
-    dc_own, dc_sib = halves(d_context, c, hw)
-    dc_recv = swap(dc_sib, 1, groups)
-    d_qkv = bwd_call(own_qkv, recv_qkv, dc_own, dc_recv, context_all, logs, qmask, kmask, idx, cnt)
-    d_own = d_qkv[: 2 * local]
-    d_sib = swap(d_qkv[2 * local :], 1, groups)
-    d_input = d_res + nt(d_own, w_own) + nt(d_sib, w_sib)
+    d_context = nt(d_attended, out_full).astype(BF)
+    dc_own = take_half(d_context, c, hw)
+    dc_recv = swap(take_half(d_context, 1 - c, hw), 1, groups)
+    proj = tn(context, d_attended)
+    proj = core_sum(take_half(proj, c, width // 2), take_half(proj, 1 - c, width // 2))
+    proj = sum_rows(proj, place, y, ["y", 0] + zs, shards, groups)
+    d_qkv = bwd_call(qkv, dc_own, dc_recv, ctx_own, ctx_give, logs, qmask, kmask, idx, cnt)
+    qkv_grad = sum_rows(tn(x_all, d_qkv).astype(BF), place, y, [0] + zs + ["y"], shards, groups)
+    give = nt(d_qkv[2 * local :], w_qkv).astype(BF)
+    d_input = d_res + nt(d_qkv[: 2 * local], w_qkv) + swap(give, 1, groups).astype(F32)
     input_grad = give_back(d_input.astype(BF))
-    joined_grad = scatter_rows(join(tn(x, d_own), tn(x, d_sib), c, hw))
-    vec = [v.reshape(shards, -1) for v in (d_bias, d_gain_one, d_shift_one, d_gain_two, d_shift_two)]
-    vec = lax.psum(lax.psum_scatter(jnp.concatenate(vec, axis=1), "shard", scatter_dimension=0, tiled=True), "seq")[0]
+
+    db = join(jnp.sum(di_own.astype(F32), axis=0)[None], jnp.sum(di_sib.astype(F32), axis=0)[None], c, frows // 2)
+    vec = [v.reshape(shards, -1) for v in (db, d_gain_one, d_shift_one, d_gain_two, d_shift_two)]
+    vec = jnp.concatenate(vec, axis=1)
+    for flip in (1, 2):
+        vec = vec + swap(vec, flip, groups)
+    for bit in range(top):
+        vec = vec + cross(vec, bit, shards)
+    vec = lax.dynamic_index_in_dim(vec, place, 0, keepdims=False)
     vecs = [vec[a:b] for a, b in zip(cuts[:-1], cuts[1:])]
+
+    joined_grad = join(qkv_grad, swap(qkv_grad, 1, groups), c, hw).astype(F32)
+    proj_grad = join(proj, swap(proj, 1, groups), c, width // 2).astype(F32)
+    inner_grad = join(in_grad, swap(in_grad, 1, groups), c, frows // 2).astype(F32)
+    back_other = swap(back_grad, 1, groups)
+    outer_grad = jnp.where(
+        c == 0, jnp.concatenate([back_grad, back_other]), jnp.concatenate([back_other, back_grad])
+    ).astype(F32)
     return (
         result,
         input_grad,
         joined_grad[:, :width],
         joined_grad[:, width : 2 * width],
         joined_grad[:, 2 * width :],
-        projection_grad,
+        proj_grad,
         inner_grad,
         vecs[0],
         outer_grad,

time: 778 us -> 549 us (0.71)
  waiting for transfers between devices: 321 us -> 126 us
  blocking collectives: 101 us -> 0 us
  starting transfers between devices: 7.86 us -> 52.1 us
  other arithmetic: 23.3 us -> 43.6 us
  Pallas kernels: 140 us -> 154 us
  between operations: 15.1 us -> 2.58 us
  local copies, waits for them, and re-layouts: 52.7 us -> 63.8 us
    reduce_scatter x4 -> x0, waiting for transfers between devices: 210 us -> none  [scatter_rows(): lax.psum_scatter(grad.astype(BF), ('shard', 'seq'), scatter_dimension=0,...]
    all_gather x4 -> x0, waiting for transfers between devices: 110 us -> none  [gather_rows(): return lax.all_gather(mine, ('shard', 'seq'), axis=0, tiled=True)]
    ppermute x0 -> x43, waiting for transfers between devices: none -> 96.6 us  [cross(): lax.ppermute(value, 'shard', [(i, i ^ 1 << bit) for i in range(shards)])]
    all_gather x5 -> x0, blocking collectives: 59.2 us -> none  [the longest x1 31 us: body(): lax.all_gather(small_local, 'shard', axis=0, tiled=False).astype(F32)]
    ppermute x0 -> x43, starting transfers between devices: none -> 41.8 us  [cross(): lax.ppermute(value, 'shard', [(i, i ^ 1 << bit) for i in range(shards)])]
    unnamed x1 -> x0, blocking collectives: 36.3 us -> none
    ppermute x8 -> x29, waiting for transfers between devices: 0.56 us -> 29.3 us  [swap(): return lax.ppermute(value, 'seq', [(s, s ^ flip) for s in range(groups)])]
    convert_element_type x4 -> x26, other arithmetic: 3.53 us -> 25.3 us  [the longest x16 6.46 us: sum_rows(): value = (keep.astype(F32) + got.astype(F32)).astype(BF)]
  transfers between devices with their start and end apart: 16 -> 72, of which waited for: 7 -> 27; matrix products, arithmetic and copies ran while one was open for 17% -> 33% of each run, Pallas kernels for 18% -> 28%
where the time goes in v2:
time: 549 us; the launch traced here: 543 us
  Pallas kernels  154 us (28%)
  waiting for transfers between devices  126 us (23%)
  matrix products  101 us (18%)
  local copies, waits for them, and re-layouts  63.8 us (12%)
  starting transfers between devices  52.1 us (9%)
  other arithmetic  43.6 us (8%)
    ppermute x43, waiting for transfers between devices, cross(): lax.ppermute(value, 'shard', [(i, i ^ 1 << bit) for i in range(shards)])  96.6 us
    pallas_call x1, Pallas kernels, bwd_call(): pl.pallas_call(kern, name='attn_bwd', out_shape=jax.ShapeDtypeStruct((seq...  88.4 us
    pallas_call x1, Pallas kernels, fwd_call(): pl.pallas_call(kern, name='attn_fwd', out_shape=(jax.ShapeDtypeStruct((ha...  54.1 us
    ppermute x43, starting transfers between devices, cross(): lax.ppermute(value, 'shard', [(i, i ^ 1 << bit) for i in range(shards)])  41.8 us
    dot_general x7, matrix products, nt(): lax.dot_general(a, b, (((1,), (1,)), ((), ())), preferred_element_type=F32)  38.2 us
    dot_general x6, matrix products, nn(): lax.dot_general(a, b, (((1,), (0,)), ((), ())), preferred_element_type=F32)  33 us
    dot_general x6, matrix products, tn(): lax.dot_general(a, b, (((0,), (0,)), ((), ())), preferred_element_type=F32)  29.8 us
    ppermute x29, waiting for transfers between devices, swap(): return lax.ppermute(value, 'seq', [(s, s ^ flip) for s in range(groups)])  29.3 us
  transfers between devices with their start and end apart: 72, of which 27 were waited for; matrix products, arithmetic and copies ran while one was open for 33% of the time, Pallas kernels for 28%

profile of v2, /device:TPU:0, one launch (start us, length us, event | category | flops | bytes accessed | tf_op | source)
XLA Modules:
  0.0 542.9 jit_solution(16720231587677787511)
XLA Ops:
  37.0 5.1 collective-permute-done.6.refs_4_
  72.7 8.6 %convolution_convert_fusion.qkv_ref = bf16[2048,1152]{1,0:T(8,128)(2,1)} fusion(bf16[768,1152]{1,0:T(8,128)(2,1)} %arrange.4, bf16[512,768]{0,1:T(8,128)(2,1)} %collective-permute-done.2, bf16[512,768]{0,1:T(8,128)(2,1)} %collective-permute-done.1, bf16[512,768]{0,1:T(8,128)(2,1)} %collective-permute-done, bf16[512,768]{0,1:T(8,128)(2,1)S(1)} %bitcast.219), kind=kOutput, calls=%fused_computation.4 | convolution fusion | flops 3638820864 | bytes 9633792 | tf_op jit(solution)/shard_map/dot_general | solution.py:16
  87.0 54.1 %attn_fwd.1 = (bf16[1024,384]{1,0:T(8,128)(2,1)}, bf16[1024,384]{1,0:T(8,128)(2,1)}, f32[4096,128]{1,0:T(8,128)}) custom-call(s32[32,32]{1,0:T(8,128)} %broadcast_add_fusion.idx_ref, s32[32]{0:T(128)} %and_select_fusion.cnt_ref, bf16[2048,1152]{1,0:T(8,128)(2,1)} %convolution_convert_fusion.qkv_ref, bf16[2048,128]{1,0:T(8,128)(2,1)} %select_convert_fusion.qm_ref, ...), custom_call_target="tpu_custom_call" | custom-call | flops 20000000000 | bytes 12000000 | tf_op jit(solution)/shard_map/attn_fwd/pallas_call | solution.py:79
  159.8 7.6 %collective-permute-done.28.refs_3_ = bf16[192,768]{1,0:T(8,128)(2,1)} collective-permute-done((bf16[192,768]{1,0:T(8,128)(2,1)}, bf16[192,768]{1,0:T(8,128)(2,1)}, u32[]{:S(2)}, u32[]{:S(2)}) %collective-permute-start.28) | collective-permute-done | bytes 294944 | tf_op jit(solution)/shard_map/ppermute | solution.py:191
  184.0 9.9 %multiply_convert_fusion = (bf16[1024,1536]{1,0:T(8,128)(2,1)S(1)}, f32[1024,1536]{1,0:T(8,128)}) fusion(f32[1536]{0:T(1024)S(1)} %add.415, bf16[1024,768]{0,1:T(8,128)(2,1)S(1)} %fusion.21, bf16[768,1536]{1,0:T(8,128)(2,1)} %collective-permute-done.33), kind=kOutput, calls=%fused_computation.21 | convolution fusion | flops 2431647744 | bytes 13375488 | tf_op jit(solution)/shard_map/dot_general | solution.py:16
  193.9 4.5 fusion.74
  213.8 8.0 %convert_reduce_fusion.1 = (f32[1536]{0:T(1024)S(1)}, bf16[1024,1536]{1,0:T(8,128)(2,1)}) fusion(f32[1024,1536]{1,0:T(8,128)S(1)} %fusion.73, f32[1536]{0:T(1024)S(1)} %add.408, bf16[1024,768]{0,1:T(8,128)(2,1)S(1)} %get-tuple-element.104, bf16[1536,768]{1,0:T(8,128)(2,1)S(1)} %copy-done.15), kind=kOutput, calls=%fused_computation.20 | convolution fusion | flops 2450520576 | bytes 13381632 | tf_op jit(solution)/shard_map/dot_general | solution.py:14
  222.4 10.1 %convert_reduce_fusion = (f32[1536]{0:T(1024)S(1)}, bf16[1024,1536]{1,0:T(8,128)(2,1)}) fusion(f32[1024,1536]{1,0:T(8,128)} %get-tuple-element.134, f32[1536]{0:T(1024)S(1)} %add.415, bf16[1024,768]{0,1:T(8,128)(2,1)} %copy-done.20, bf16[1536,768]{1,0:T(8,128)(2,1)} %collective-permute-done.34), kind=kOutput, calls=%fused_computation.19 | convolution fusion | flops 2450520576 | bytes 13381632 | tf_op jit(solution)/shard_map/dot_general | solution.py:14
  232.7 6.5 %convolution_convert_fusion.2 = bf16[768,1536]{1,0:T(8,128)(2,1)} fusion(bf16[1024,768]{0,1:T(8,128)(2,1)} %copy-done.18, bf16[1024,1536]{1,0:T(8,128)(2,1)} %get-tuple-element.139), kind=kOutput, calls=%fused_computation.32 | convolution fusion | flops 2417098752 | bytes 7077888 | tf_op jit(solution)/shard_map/dot_general | solution.py:15
  239.3 4.4 fusion.75
  243.8 6.8 %multiply_reduce_fusion = (f32[768]{0:T(1024)S(1)}, f32[1024]{0:T(1024)S(1)}, f32[1024]{0:T(1024)S(1)}, f32[768]{0:T(1024)S(1)}, f32[1024,768]{0,1:T(8,128)}) fusion(f32[1024,768]{0,1:T(8,128)S(1)} %get-tuple-element.99, f32[1024]{0:T(1024)S(1)} %add_rsqrt_fusion.1, f32[1024]{0:T(1024)S(1)} %broadcast_multiply_fusion.5, f32[768]{0:T(1024)S(1)} %mul.211, ...), kind=kOutput, calls=%fused_computation.39 | convolution fusion | flops 2433217024 | bytes 19705856 | tf_op jit(solution)/shard_map/dot_general | solution.py:14
  280.7 88.4 %attn_bwd.1 = bf16[2048,1152]{1,0:T(8,128)(2,1)} custom-call(s32[32,32]{1,0:T(8,128)} %broadcast_add_fusion.idx_ref, s32[32]{0:T(128)} %and_select_fusion.cnt_ref, bf16[2048,1152]{1,0:T(8,128)(2,1)} %convolution_convert_fusion.qkv_ref, bf16[1024,384]{1,0:T(8,128)(2,1)} %bitcast.222, bf16[1024,384]{1,0:T(8,128)(2,1)} %collective-permute-done.37.dr_ref, ...), custom_call_target="tpu_custom_call" | custom-call | flops 49999998976 | bytes 18000000 | tf_op jit(solution)/shard_map/attn_bwd/pallas_call | solution.py:151
  369.1 7.6 %convolution_convert_fusion.3 = bf16[768,1152]{1,0:T(8,128)(2,1)S(1)} fusion(bf16[2048,1152]{1,0:T(8,128)(2,1)} %attn_bwd.1, bf16[512,768]{0,1:T(8,128)(2,1)} %collective-permute-done.2, bf16[512,768]{0,1:T(8,128)(2,1)} %collective-permute-done.1, bf16[512,768]{0,1:T(8,128)(2,1)} %collective-permute-done, bf16[512,768]{0,1:T(8,128)(2,1)} %bitcast.218), kind=kOutput, calls=%fused_computation.33 | convolution fusion | flops 3637346304 | bytes 9633792 | tf_op jit(solution)/shard_map/dot_general | solution.py:15
  383.2 4.4 collective-permute-done.48
  392.2 13.1 %collective-permute-done.40 = bf16[2,2,2,48,1152]{4,3,2,0,1:T(8,128)(2,1)S(1)} collective-permute-done((bf16[2,2,2,48,1152]{4,3,2,0,1:T(8,128)(2,1)S(1)}, bf16[2,2,2,48,1152]{4,3,2,0,1:T(8,128)(2,1)S(1)}, u32[]{:S(2)}, u32[]{:S(2)}) %collective-permute-start.40) | collective-permute-done | bytes 884768 | tf_op jit(solution)/shard_map/ppermute | solution.py:191
  415.7 4.5 collective-permute-done.41
  424.5 7.0 %collective-permute-done.42 = bf16[2,48,1152]{2,1,0:T(8,128)(2,1)S(1)} collective-permute-done((bf16[2,48,1152]{2,1,0:T(8,128)(2,1)S(1)}, bf16[2,48,1152]{2,1,0:T(8,128)(2,1)S(1)}, u32[]{:S(2)}, u32[]{:S(2)}) %collective-permute-start.42) | collective-permute-done | bytes 221216 | tf_op jit(solution)/shard_map/ppermute | solution.py:191
  436.9 6.2 %add_convert_fusion = bf16[1536,768]{1,0:T(8,128)(2,1)S(1)} fusion(bf16[1536,768]{1,0:T(8,128)(2,1)} %collective-permute-done.65, bf16[1024,768]{0,1:T(8,128)(2,1)S(1)} %copy-done.21, f32[1024,1536]{1,0:T(8,128)S(1)} %bitcast.236, f32[1536]{0:T(1024)S(1)} %add.408), kind=kOutput, calls=%fused_computation.26 | convolution fusion | flops 2435186688 | bytes 12589056 | tf_op jit(solution)/shard_map/dot_general | solution.py:15
  453.1 20.0 %collective-permute-done.44 = bf16[48,1152]{1,0:T(8,128)(2,1)S(1)} collective-permute-done((bf16[48,1152]{1,0:T(8,128)(2,1)S(1)}, bf16[48,1152]{1,0:T(8,128)(2,1)S(1)}, u32[]{:S(2)}, u32[]{:S(2)}) %collective-permute-start.44) | collective-permute-done | bytes 110624 | tf_op jit(solution)/shard_map/ppermute | solution.py:187
  482.8 11.5 %collective-permute-done.67 = bf16[2,2,96,768]{3,2,0,1:T(8,128)(2,1)S(1)} collective-permute-done((bf16[2,2,96,768]{3,2,0,1:T(8,128)(2,1)S(1)}, bf16[2,2,96,768]{3,2,0,1:T(8,128)(2,1)S(1)}, u32[]{:S(2)}, u32[]{:S(2)}) %collective-permute-start.67) | collective-permute-done | bytes 589856 | tf_op jit(solution)/shard_map/ppermute | solution.py:191
  499.0 9.4 %collective-permute-done.68 = bf16[2,96,768]{2,1,0:T(8,128)(2,1)S(1)} collective-permute-done((bf16[2,96,768]{2,1,0:T(8,128)(2,1)S(1)}, bf16[2,96,768]{2,1,0:T(8,128)(2,1)S(1)}, u32[]{:S(2)}, u32[]{:S(2)}) %collective-permute-start.68) | collective-permute-done | bytes 294944 | tf_op jit(solution)/shard_map/ppermute | solution.py:191
  508.6 8.4 %collective-permute-done.56 = bf16[2,48,1536]{2,1,0:T(8,128)(2,1)S(1)} collective-permute-done((bf16[2,48,1536]{2,1,0:T(8,128)(2,1)S(1)}, bf16[2,48,1536]{2,1,0:T(8,128)(2,1)S(1)}, u32[]{:S(2)}, u32[]{:S(2)}) %collective-permute-start.56) | collective-permute-done | bytes 294944 | tf_op jit(solution)/shard_map/ppermute | solution.py:191
  519.6 4.3 collective-permute-done.57
  533.4 5.2 fusion.38
  (427 shorter events, 224.7 us)
Async XLA Ops:
  5.4 22.4 %collective-permute-start.14 = (bf16[112,384]{1,0:T(8,128)(2,1)S(1)}, bf16[112,384]{1,0:T(8,128)(2,1)}, u32[]{:S(2)}, u32[]{:S(2)}) collective-permute-start(bf16[112,384]{1,0:T(8,128)(2,1)S(1)} %pad_maximum_fusion.5.refs_0_), channel_id=1, source_target_pairs={{0,16},{4,20},{8,24},{12,28},{16,0},{20,4},{24,8},{28,12},{1,17},{... | collective-permute-start | bytes 258056 | tf_op jit(solution)/shard_map/ppermute | solution.py:191
  11.1 19.8 %collective-permute-start.11 = (bf16[112,384]{1,0:T(8,128)(2,1)S(1)}, bf16[112,384]{1,0:T(8,128)(2,1)}, u32[]{:S(2)}, u32[]{:S(2)}) collective-permute-start(bf16[112,384]{1,0:T(8,128)(2,1)S(1)} %pad_maximum_fusion.5.refs_0_), channel_id=1, source_target_pairs={{0,4},{4,0},{8,12},{12,8},{16,20},{20,16},{24,28},{28,24},{1,5},{5... | collective-permute-start | bytes 258056 | tf_op jit(solution)/shard_map/ppermute | solution.py:191
  35.0 35.6 %collective-permute-start.1 = (bf16[512,768]{0,1:T(8,128)(2,1)}, bf16[512,768]{0,1:T(8,128)(2,1)}, u32[]{:S(2)}, u32[]{:S(2)}) collective-permute-start(bf16[512,768]{0,1:T(8,128)(2,1)} %bitcast.216), channel_id=1, source_target_pairs={{0,1},{1,0},{2,3},{3,2},{4,5},{5,4},{6,7},{7,6},{8,9},{9,8},{10,11... | collective-permute-start | bytes 2359304 | tf_op jit(solution)/shard_map/ppermute | solution.py:187
  36.7 34.0 %collective-permute-start.2 = (bf16[512,768]{0,1:T(8,128)(2,1)}, bf16[512,768]{0,1:T(8,128)(2,1)}, u32[]{:S(2)}, u32[]{:S(2)}) collective-permute-start(bf16[512,768]{0,1:T(8,128)(2,1)} %collective-permute-done), channel_id=1, source_target_pairs={{0,1},{1,0},{2,3},{3,2},{4,5},{5,4},{6,7},{7,6},{8,9},{9,8},{10,11... | collective-permute-start | bytes 2359304 | tf_op jit(solution)/shard_map/ppermute | solution.py:187
  69.5 71.6 %collective-permute-start.29 = (bf16[192,768]{1,0:T(8,128)(2,1)S(1)}, bf16[192,768]{1,0:T(8,128)(2,1)S(1)}, u32[]{:S(2)}, u32[]{:S(2)}) collective-permute-start(bf16[192,768]{1,0:T(8,128)(2,1)S(1)} %constant_dynamic-slice_fusion.10.refs_0_), channel_id=1, source_target_pairs={{0,16},{4,20},{8,24},{12,28},{16,0},{20,4},{24,8},{28,12},{1,17},{... | collective-permute-start | bytes 884744 | tf_op jit(solution)/shard_map/ppermute | solution.py:191
  70.7 85.4 %collective-permute-start.18 = (bf16[768,384]{1,0:T(8,128)(2,1)S(1)}, bf16[768,384]{1,0:T(8,128)(2,1)S(1)}, u32[]{:S(2)}, u32[]{:S(2)}) collective-permute-start(bf16[768,384]{1,0:T(8,128)(2,1)S(1)} %bitcast.196), channel_id=1, source_target_pairs={{0,1},{1,0},{2,3},{3,2},{4,5},{5,4},{6,7},{7,6},{8,9},{9,8},{10,11... | collective-permute-start | bytes 1769480 | tf_op jit(solution)/shard_map/ppermute | solution.py:187
  81.3 60.0 %collective-permute-start.23 = (bf16[96,1536]{1,0:T(8,128)(2,1)S(1)}, bf16[96,1536]{1,0:T(8,128)(2,1)S(1)}, u32[]{:S(2)}, u32[]{:S(2)}) collective-permute-start(bf16[96,1536]{1,0:T(8,128)(2,1)S(1)} %collective-permute-done.22.refs_4_), channel_id=1, source_target_pairs={{0,4},{4,0},{8,12},{12,8},{16,20},{20,16},{24,28},{28,24},{1,5},{5... | collective-permute-start | bytes 884744 | tf_op jit(solution)/shard_map/ppermute | solution.py:191
  82.7 58.5 %collective-permute-start.21 = (bf16[96,1536]{1,0:T(8,128)(2,1)S(1)}, bf16[96,1536]{1,0:T(8,128)(2,1)}, u32[]{:S(2)}, u32[]{:S(2)}) collective-permute-start(bf16[96,1536]{1,0:T(8,128)(2,1)S(1)} %collective-permute-done.20.refs_2_), channel_id=1, source_target_pairs={{0,4},{4,0},{8,12},{12,8},{16,20},{20,16},{24,28},{28,24},{1,5},{5... | collective-permute-start | bytes 884744 | tf_op jit(solution)/shard_map/ppermute | solution.py:191
  86.0 57.3 %collective-permute-start.25 = (bf16[96,1536]{1,0:T(8,128)(2,1)}, bf16[96,1536]{1,0:T(8,128)(2,1)S(1)}, u32[]{:S(2)}, u32[]{:S(2)}) collective-permute-start(bf16[96,1536]{1,0:T(8,128)(2,1)} %collective-permute-done.24.refs_6_), channel_id=1, source_target_pairs={{0,4},{4,0},{8,12},{12,8},{16,20},{20,16},{24,28},{28,24},{1,5},{5... | collective-permute-start | bytes 884744 | tf_op jit(solution)/shard_map/ppermute | solution.py:191
  144.0 29.6 %collective-permute-start.10 = (bf16[1024,384]{1,0:T(8,128)(2,1)}, bf16[1024,384]{1,0:T(8,128)(2,1)S(1)}, u32[]{:S(2)}, u32[]{:S(2)}) collective-permute-start(bf16[1024,384]{1,0:T(8,128)(2,1)} %get-tuple-element.17.or_ref), channel_id=1, source_target_pairs={{0,1},{1,0},{2,3},{3,2},{4,5},{5,4},{6,7},{7,6},{8,9},{9,8},{10,11... | collective-permute-start | bytes 2359304 | tf_op jit(solution)/shard_map/ppermute | solution.py:187
  156.0 27.9 %collective-permute-start.33 = (bf16[768,1536]{1,0:T(8,128)(2,1)}, bf16[768,1536]{1,0:T(8,128)(2,1)}, u32[]{:S(2)}, u32[]{:S(2)}) collective-permute-start(bf16[768,1536]{1,0:T(8,128)(2,1)} %arrange.6), channel_id=1, source_target_pairs={{0,1},{1,0},{2,3},{3,2},{4,5},{5,4},{6,7},{7,6},{8,9},{9,8},{10,11... | collective-permute-start | bytes 7077896 | tf_op jit(solution)/shard_map/ppermute | solution.py:187
  167.3 35.2 %collective-permute-start.36 = (bf16[512,768]{0,1:T(8,128)(2,1)}, bf16[512,768]{0,1:T(8,128)(2,1)}, u32[]{:S(2)}, u32[]{:S(2)}) collective-permute-start(bf16[512,768]{0,1:T(8,128)(2,1)} %bitcast.22), channel_id=1, source_target_pairs={{0,2},{1,3},{2,0},{3,1},{4,6},{5,7},{6,4},{7,5},{8,10},{9,11},{10,... | collective-permute-start | bytes 2359304 | tf_op jit(solution)/shard_map/ppermute | solution.py:187
  173.6 20.2 %collective-permute-start.34 = (bf16[1536,768]{1,0:T(8,128)(2,1)}, bf16[1536,768]{1,0:T(8,128)(2,1)}, u32[]{:S(2)}, u32[]{:S(2)}) collective-permute-start(bf16[1536,768]{1,0:T(8,128)(2,1)} %arrange.7), channel_id=1, source_target_pairs={{0,1},{1,0},{2,3},{3,2},{4,5},{5,4},{6,7},{7,6},{8,9},{9,8},{10,11... | collective-permute-start | bytes 7077896 | tf_op jit(solution)/shard_map/ppermute | solution.py:187
  221.9 215.0 %collective-permute-start.65 = (bf16[1536,768]{1,0:T(8,128)(2,1)}, bf16[1536,768]{1,0:T(8,128)(2,1)}, u32[]{:S(2)}, u32[]{:S(2)}) collective-permute-start(bf16[1536,768]{1,0:T(8,128)(2,1)} %convolution_convert_fusion.1), channel_id=1, source_target_pairs={{0,1},{1,0},{2,3},{3,2},{4,5},{5,4},{6,7},{7,6},{8,9},{9,8},{10,11... | collective-permute-start | bytes 7077896 | tf_op jit(solution)/shard_map/ppermute | solution.py:187
  251.0 194.3 %collective-permute-start.53 = (bf16[768,1536]{1,0:T(8,128)(2,1)}, bf16[768,1536]{1,0:T(8,128)(2,1)}, u32[]{:S(2)}, u32[]{:S(2)}) collective-permute-start(bf16[768,1536]{1,0:T(8,128)(2,1)} %convolution_convert_fusion.2), channel_id=1, source_target_pairs={{0,1},{1,0},{2,3},{3,2},{4,5},{5,4},{6,7},{7,6},{8,9},{9,8},{10,11... | collective-permute-start | bytes 7077896 | tf_op jit(solution)/shard_map/ppermute | solution.py:187
  274.3 135.9 %collective-permute-start.35 = (bf16[512,768]{0,1:T(8,128)(2,1)}, bf16[512,768]{0,1:T(8,128)(2,1)}, u32[]{:S(2)}, u32[]{:S(2)}) collective-permute-start(bf16[512,768]{0,1:T(8,128)(2,1)} %get-tuple-element.117), channel_id=1, source_target_pairs={{0,2},{1,3},{2,0},{3,1},{4,6},{5,7},{6,4},{7,5},{8,10},{9,11},{10,... | collective-permute-start | bytes 2359304 | tf_op jit(solution)/shard_map/ppermute | solution.py:187
  278.7 102.1 %collective-permute-start.47 = (bf16[2,2,2,48,384]{4,3,2,1,0:T(8,128)(2,1)}, bf16[2,2,2,48,384]{4,3,2,1,0:T(8,128)(2,1)S(1)}, u32[]{:S(2)}, u32[]{:S(2)}) collective-permute-start(bf16[2,2,2,48,384]{4,3,2,1,0:T(8,128)(2,1)} %dynamic-slice_bitcast_fusion.6), channel_id=1, source_target_pairs={{0,2},{1,3},{2,0},{3,1},{4,6},{5,7},{6,4},{7,5},{8,10},{9,11},{10,... | collective-permute-start | bytes 884744 | tf_op jit(solution)/shard_map/ppermute | solution.py:187
  381.2 24.1 %collective-permute-start.40 = (bf16[2,2,2,48,1152]{4,3,2,0,1:T(8,128)(2,1)S(1)}, bf16[2,2,2,48,1152]{4,3,2,0,1:T(8,128)(2,1)S(1)}, u32[]{:S(2)}, u32[]{:S(2)}) collective-permute-start(bf16[2,2,2,48,1152]{4,3,2,0,1:T(8,128)(2,1)S(1)} %bitcast.211), channel_id=1, source_target_pairs={{0,4},{4,0},{8,12},{12,8},{16,20},{20,16},{24,28},{28,24},{1,5},{5... | collective-permute-start | bytes 2654216 | tf_op jit(solution)/shard_map/ppermute | solution.py:191
  392.1 40.6 %collective-permute-start.38 = (bf16[1024,768]{0,1:T(8,128)(2,1)}, bf16[1024,768]{0,1:T(8,128)(2,1)}, u32[]{:S(2)}, u32[]{:S(2)}) collective-permute-start(bf16[1024,768]{0,1:T(8,128)(2,1)} %fusion.29), channel_id=1, source_target_pairs={{0,1},{1,0},{2,3},{3,2},{4,5},{5,4},{6,7},{7,6},{8,9},{9,8},{10,11... | collective-permute-start | bytes 4718600 | tf_op jit(solution)/shard_map/ppermute | solution.py:187
  444.5 32.6 %collective-permute-start.66 = (bf16[2,2,2,96,768]{4,3,0,1,2:T(8,128)(2,1)}, bf16[2,2,2,96,768]{4,3,0,1,2:T(8,128)(2,1)}, u32[]{:S(2)}, u32[]{:S(2)}) collective-permute-start(bf16[2,2,2,96,768]{4,3,0,1,2:T(8,128)(2,1)} %bitcast.186), channel_id=1, source_target_pairs={{0,2},{1,3},{2,0},{3,1},{4,6},{5,7},{6,4},{7,5},{8,10},{9,11},{10,... | collective-permute-start | bytes 3538952 | tf_op jit(solution)/shard_map/ppermute | solution.py:187
  450.1 23.0 %collective-permute-start.44 = (bf16[48,1152]{1,0:T(8,128)(2,1)S(1)}, bf16[48,1152]{1,0:T(8,128)(2,1)S(1)}, u32[]{:S(2)}, u32[]{:S(2)}) collective-permute-start(bf16[48,1152]{1,0:T(8,128)(2,1)S(1)} %fusion.51), channel_id=1, source_target_pairs={{0,2},{1,3},{2,0},{3,1},{4,6},{5,7},{6,4},{7,5},{8,10},{9,11},{10,... | collective-permute-start | bytes 331784 | tf_op jit(solution)/shard_map/ppermute | solution.py:187
  452.1 28.1 %collective-permute-start.54 = (bf16[2,2,2,48,1536]{4,3,2,1,0:T(8,128)(2,1)}, bf16[2,2,2,48,1536]{4,3,2,1,0:T(8,128)(2,1)}, u32[]{:S(2)}, u32[]{:S(2)}) collective-permute-start(bf16[2,2,2,48,1536]{4,3,2,1,0:T(8,128)(2,1)} %dynamic-slice_bitcast_fusion), channel_id=1, source_target_pairs={{0,4},{4,0},{8,12},{12,8},{16,20},{20,16},{24,28},{28,24},{1,5},{5... | collective-permute-start | bytes 3538952 | tf_op jit(solution)/shard_map/ppermute | solution.py:191
  474.5 49.9 %collective-permute-start.39 = (bf16[512,768]{0,1:T(8,128)(2,1)}, bf16[512,768]{0,1:T(8,128)(2,1)}, u32[]{:S(2)}, u32[]{:S(2)}) collective-permute-start(bf16[512,768]{0,1:T(8,128)(2,1)} %get-tuple-element.111), channel_id=1, source_target_pairs={{0,2},{1,3},{2,0},{3,1},{4,6},{5,7},{6,4},{7,5},{8,10},{9,11},{10,... | collective-permute-start | bytes 2359304 | tf_op jit(solution)/shard_map/ppermute | solution.py:187
  497.6 19.4 %collective-permute-start.56 = (bf16[2,48,1536]{2,1,0:T(8,128)(2,1)S(1)}, bf16[2,48,1536]{2,1,0:T(8,128)(2,1)S(1)}, u32[]{:S(2)}, u32[]{:S(2)}) collective-permute-start(bf16[2,48,1536]{2,1,0:T(8,128)(2,1)S(1)} %dynamic-slice_bitcast_fusion.5), channel_id=1, source_target_pairs={{0,16},{4,20},{8,24},{12,28},{16,0},{20,4},{24,8},{28,12},{1,17},{... | collective-permute-start | bytes 884744 | tf_op jit(solution)/shard_map/ppermute | solution.py:191
  (103 other events, 1117.9 us)
